TPU v7x, 128 devices: a whole 4x4x4 slice. The times are simulated.
128 devices in a mesh: facet: 16 (over x, y), sub: 8 (over z, core).
Axes of the slice: x: 4, y: 4, z: 4, core: 2. Of those that a mesh axis runs over, the one named last changes fastest.
Arguments:
- strips: bfloat16 [16, 64, 8192], P('facet', 'sub'), may hold values from -6 to 6
- facet_offset: int32 [16], replicated, may hold values from 0 to 448
- subgrid_offset: int32 [128], replicated, may hold values from 0 to 4095
- owner: int32 [128], replicated, may hold values from 0 to 127, as said below
- screen_index: int32 [128], replicated, may hold values from 0 to 15
- screens: bfloat16 [16, 64, 1024], replicated, may hold values from -1 to 1, as said below
- grid_weight: float32 [512, 512], P(('facet', 'sub')), may hold values from 0.3 to 3
Outputs:
- facet_out: float32 [16, 64, 8192], P('facet', 'sub')
Inputs may be any that keep to these rules, and one draw needn't show every extreme that they name: `owner`: device number i * 8 + k is the device at index i of facet and k of sub. No device owns more than 4 subgrids, and some device owns exactly 4. `screens`: element g and element 512 + g of a row are the cosine and sine of one phase.
All inputs are finite; a program needn't handle non-finite values.
Results may differ from a plain program's by a relative error of at most 0.0059.
Values may be sent and summed in bfloat16 or wider, within the bound.
A program may use at most 64 MiB of HBM per device.

v0:
```python
import math

import jax
import jax.numpy as jnp
from jax import lax
from jax.sharding import PartitionSpec as P

FL = 4096
M = 64
SG = 512
W = 8
CAP = 4


def table_block(start, length, count):
    points = jnp.arange(length, dtype=jnp.int32)
    orders = start + jnp.arange(count, dtype=jnp.int32)
    turn_counts = points[:, None] * orders[None, :] % length
    angles = turn_counts.astype(jnp.float32) * (2.0 * math.pi / length)
    factor = 1.0 / math.sqrt(length)
    cosine = jnp.cos(angles) * factor
    sine_part = jnp.sin(angles) * factor
    upper = jnp.concatenate([cosine, -sine_part], axis=1)
    lower = jnp.concatenate([sine_part, cosine], axis=1)
    return jnp.concatenate([upper, lower], axis=0).astype(jnp.bfloat16)


def full_spectrum(rows):
    width = min(FL, 512)
    blocks = FL // width
    row_count = rows.shape[0]

    def one_block(index):
        block = table_block(index * width, FL, width)
        product = jnp.dot(rows, block, preferred_element_type=jnp.float32)
        return product.astype(jnp.bfloat16).reshape(row_count, 2, width)

    pieces = lax.map(one_block, jnp.arange(blocks, dtype=jnp.int32))
    return jnp.transpose(pieces, (1, 2, 0, 3)).reshape(row_count, 2 * FL)


def synthesize(spectrum):
    width = min(FL, 512)
    blocks = FL // width
    row_count = spectrum.shape[0]
    shaped = spectrum.reshape(row_count, 2, blocks, width)

    def add_block(index, accumulated):
        block = table_block(index * width, FL, width)
        piece = lax.dynamic_index_in_dim(shaped, index, 2, keepdims=False).reshape(
            row_count, 2 * width
        )
        return accumulated + lax.dot_general(
            piece, block, (((1,), (1,)), ((), ())), preferred_element_type=jnp.float32
        )

    return lax.fori_loop(
        jnp.int32(0), jnp.int32(blocks), add_block, jnp.zeros((row_count, 2 * FL), jnp.float32)
    )


def send_forward(buffer):
    return lax.all_to_all(buffer, ("facet", "sub"), split_axis=0, concat_axis=0, tiled=True)


def send_back(buffer):
    return lax.all_to_all(buffer, ("facet", "sub"), split_axis=0, concat_axis=0, tiled=True)


def serve_subgrids(arrived, placement, screen_rows, weight_rows, facet_count, strip_count):
    slot_count = weight_rows.shape[0]
    shaped = arrived.reshape(facet_count, strip_count, slot_count, W, 2, M)
    subgrid_sum = jnp.einsum(
        "fskwrm,fmg->kswrg", shaped, placement, preferred_element_type=jnp.float32
    )
    screen_f = screen_rows.reshape(slot_count, strip_count, W, 2, SG).astype(jnp.float32)
    weighting = weight_rows[:, None, None, :]
    real_part = (
        subgrid_sum[:, :, :, 0] * screen_f[:, :, :, 0]
        - subgrid_sum[:, :, :, 1] * screen_f[:, :, :, 1]
    ) * weighting
    imag_part = (
        subgrid_sum[:, :, :, 0] * screen_f[:, :, :, 1]
        + subgrid_sum[:, :, :, 1] * screen_f[:, :, :, 0]
    ) * weighting
    processed = jnp.stack([real_part, imag_part], axis=3).astype(jnp.bfloat16)
    extracted = jnp.einsum(
        "kswrg,fmg->fskwrm", processed, placement, preferred_element_type=jnp.float32
    )
    return extracted.astype(jnp.bfloat16).reshape(facet_count * strip_count, slot_count, W, 2 * M)


def local(strips, facet_offset, subgrid_offset, owner, screen_index, screens, grid_weight):
    facet_count = lax.axis_size("facet")
    strip_count = lax.axis_size("sub")
    subgrid_total = owner.shape[0]
    facet_here = lax.axis_index("facet")
    my_index = facet_here * strip_count + lax.axis_index("sub")
    my_offset = facet_offset[facet_here]
    order_ids = jnp.arange(M, dtype=jnp.int32)
    chosen_freq = (subgrid_offset[:, None] + my_offset + order_ids[None, :]) % FL
    spectrum = full_spectrum(strips[0])
    real_part = spectrum[:, chosen_freq]
    imag_part = spectrum[:, FL + chosen_freq]
    contributions = jnp.transpose(jnp.concatenate([real_part, imag_part], axis=2), (1, 0, 2))
    frequency_ids = jnp.arange(SG, dtype=jnp.int32)
    placement = (
        frequency_ids[None, None, :] == facet_offset[:, None, None] + order_ids[None, :, None]
    ).astype(jnp.bfloat16)
    device_ids = jnp.arange(subgrid_total, dtype=jnp.int32)
    onehot = (owner[:, None] == device_ids[None, :]).astype(jnp.int32)
    before = jnp.cumsum(onehot, axis=0) - onehot
    slot = jnp.sum(before * onehot, axis=1)
    target = owner * CAP + slot
    outgoing = (
        jnp.zeros((subgrid_total * CAP, W, 2 * M), jnp.bfloat16).at[target].set(contributions)
    )
    arrived = send_forward(outgoing.reshape(subgrid_total, CAP, W, 2 * M))
    slot_ids = jnp.arange(CAP, dtype=jnp.int32)
    picked = ((owner == my_index)[None, :] & (slot[None, :] == slot_ids[:, None])).astype(jnp.int32)
    held_subgrid = jnp.sum(picked * device_ids[None, :], axis=1)
    screen_rows = screens[screen_index[held_subgrid]]
    answer = serve_subgrids(arrived, placement, screen_rows, grid_weight, facet_count, strip_count)
    coming_back = send_back(answer)
    returned = coming_back.reshape(subgrid_total * CAP, W, 2 * M)[target]
    rows_f = jnp.transpose(returned.astype(jnp.float32), (1, 0, 2))
    back = jnp.zeros((W, 2, FL), jnp.float32)
    back = back.at[:, 0, chosen_freq].add(rows_f[:, :, :M])
    back = back.at[:, 1, chosen_freq].add(rows_f[:, :, M:])
    accumulated = synthesize(back.reshape(W, 2 * FL).astype(jnp.bfloat16))
    return accumulated[None]


def solution(mesh):
    in_specs = (P("facet", "sub", None), P(), P(), P(), P(), P(), P(("facet", "sub"), None))
    out_specs = P("facet", "sub", None)
    return jax.shard_map(local, mesh=mesh, in_specs=in_specs, out_specs=out_specs, check_vma=False)
```

profile of v0, /device:TPU:1, one launch (start us, length us, event | category | flops | bytes accessed | tf_op | source)
XLA Modules:
  0.0 1258.3 jit_solution(4868901214559270873)
XLA Ops:
  2.6 433.5 %while.25 = (s32[]{:T(128)}, bf16[8,8,2,512]{3,1,2,0:T(8,128)(2,1)S(1)}, s32[8]{0:T(128)S(1)}, bf16[8,8192]{1,0:T(8,128)(2,1)}, s32[]{:T(128)}, /*index=5*/s32[1]{0:T(128)}) while((s32[]{:T(128)}, bf16[8,8,2,512]{3,1,2,0:T(8,128)(2,1)S(1)}, s32[8]{0:T(128)S(1)}, bf16[8,8192]{1,0:T(8,128)(2,1)}, s32[]{:T(128)}, /*index=5*/s32[1]{0:T(128)}) %tuple.77), condition=%wide.region_3.4_spmd, body=%wide.region_2.3_spmd.sunk | while | flops 243278336 | bytes 25874568 | solution.py:38
  4.0 37.2 %negate_convert_fusion.4 = (bf16[4096,512]{1,0:T(8,128)(2,1)}, bf16[4096,512]{1,0:T(8,128)(2,1)}, bf16[4096,512]{1,0:T(8,128)(2,1)}) fusion(s32[512]{0:T(512)S(1)} %iota_add_fusion.5), kind=kLoop, calls=%fused_computation.22.clone.1 | loop fusion | flops 41943040 | bytes 12584960 | tf_op jit(solution)/shard_map/convert.5
  41.2 15.5 %fusion.83 = bf16[1024,8]{0,1:T(8,128)(2,1)S(1)} fusion(bf16[8,8192]{1,0:T(8,128)(2,1)S(1)} %copy-done.10, bf16[4096,512]{1,0:T(8,128)(2,1)} %get-tuple-element.209, bf16[4096,512]{1,0:T(8,128)(2,1)} %get-tuple-element.210, bf16[4096,512]{1,0:T(8,128)(2,1)} %get-tuple-element.211), kind=kOutput, calls=%fused_computation.29.clone.1 | convolution fusion | flops 201334784 | bytes 12730368 | tf_op jit(solution)/shard_map/while/body/eval_jaxpr/dot_general | solution.py:35
  58.2 37.2 %negate_convert_fusion.4 = (bf16[4096,512]{1,0:T(8,128)(2,1)}, bf16[4096,512]{1,0:T(8,128)(2,1)}, bf16[4096,512]{1,0:T(8,128)(2,1)}) fusion(s32[512]{0:T(512)S(1)} %iota_add_fusion.5), kind=kLoop, calls=%fused_computation.22.clone.1 | loop fusion | flops 41943040 | bytes 12584960 | tf_op jit(solution)/shard_map/convert.5
  95.4 15.5 %fusion.83 = bf16[1024,8]{0,1:T(8,128)(2,1)S(1)} fusion(bf16[8,8192]{1,0:T(8,128)(2,1)S(1)} %copy-done.10, bf16[4096,512]{1,0:T(8,128)(2,1)} %get-tuple-element.209, bf16[4096,512]{1,0:T(8,128)(2,1)} %get-tuple-element.210, bf16[4096,512]{1,0:T(8,128)(2,1)} %get-tuple-element.211), kind=kOutput, calls=%fused_computation.29.clone.1 | convolution fusion | flops 201334784 | bytes 12730368 | tf_op jit(solution)/shard_map/while/body/eval_jaxpr/dot_general | solution.py:35
  112.3 37.2 %negate_convert_fusion.4 = (bf16[4096,512]{1,0:T(8,128)(2,1)}, bf16[4096,512]{1,0:T(8,128)(2,1)}, bf16[4096,512]{1,0:T(8,128)(2,1)}) fusion(s32[512]{0:T(512)S(1)} %iota_add_fusion.5), kind=kLoop, calls=%fused_computation.22.clone.1 | loop fusion | flops 41943040 | bytes 12584960 | tf_op jit(solution)/shard_map/convert.5
  149.6 15.5 %fusion.83 = bf16[1024,8]{0,1:T(8,128)(2,1)S(1)} fusion(bf16[8,8192]{1,0:T(8,128)(2,1)S(1)} %copy-done.10, bf16[4096,512]{1,0:T(8,128)(2,1)} %get-tuple-element.209, bf16[4096,512]{1,0:T(8,128)(2,1)} %get-tuple-element.210, bf16[4096,512]{1,0:T(8,128)(2,1)} %get-tuple-element.211), kind=kOutput, calls=%fused_computation.29.clone.1 | convolution fusion | flops 201334784 | bytes 12730368 | tf_op jit(solution)/shard_map/while/body/eval_jaxpr/dot_general | solution.py:35
  166.5 37.2 %negate_convert_fusion.4 = (bf16[4096,512]{1,0:T(8,128)(2,1)}, bf16[4096,512]{1,0:T(8,128)(2,1)}, bf16[4096,512]{1,0:T(8,128)(2,1)}) fusion(s32[512]{0:T(512)S(1)} %iota_add_fusion.5), kind=kLoop, calls=%fused_computation.22.clone.1 | loop fusion | flops 41943040 | bytes 12584960 | tf_op jit(solution)/shard_map/convert.5
  203.8 15.5 %fusion.83 = bf16[1024,8]{0,1:T(8,128)(2,1)S(1)} fusion(bf16[8,8192]{1,0:T(8,128)(2,1)S(1)} %copy-done.10, bf16[4096,512]{1,0:T(8,128)(2,1)} %get-tuple-element.209, bf16[4096,512]{1,0:T(8,128)(2,1)} %get-tuple-element.210, bf16[4096,512]{1,0:T(8,128)(2,1)} %get-tuple-element.211), kind=kOutput, calls=%fused_computation.29.clone.1 | convolution fusion | flops 201334784 | bytes 12730368 | tf_op jit(solution)/shard_map/while/body/eval_jaxpr/dot_general | solution.py:35
  220.7 37.2 %negate_convert_fusion.4 = (bf16[4096,512]{1,0:T(8,128)(2,1)}, bf16[4096,512]{1,0:T(8,128)(2,1)}, bf16[4096,512]{1,0:T(8,128)(2,1)}) fusion(s32[512]{0:T(512)S(1)} %iota_add_fusion.5), kind=kLoop, calls=%fused_computation.22.clone.1 | loop fusion | flops 41943040 | bytes 12584960 | tf_op jit(solution)/shard_map/convert.5
  257.9 15.5 %fusion.83 = bf16[1024,8]{0,1:T(8,128)(2,1)S(1)} fusion(bf16[8,8192]{1,0:T(8,128)(2,1)S(1)} %copy-done.10, bf16[4096,512]{1,0:T(8,128)(2,1)} %get-tuple-element.209, bf16[4096,512]{1,0:T(8,128)(2,1)} %get-tuple-element.210, bf16[4096,512]{1,0:T(8,128)(2,1)} %get-tuple-element.211), kind=kOutput, calls=%fused_computation.29.clone.1 | convolution fusion | flops 201334784 | bytes 12730368 | tf_op jit(solution)/shard_map/while/body/eval_jaxpr/dot_general | solution.py:35
  274.9 37.2 %negate_convert_fusion.4 = (bf16[4096,512]{1,0:T(8,128)(2,1)}, bf16[4096,512]{1,0:T(8,128)(2,1)}, bf16[4096,512]{1,0:T(8,128)(2,1)}) fusion(s32[512]{0:T(512)S(1)} %iota_add_fusion.5), kind=kLoop, calls=%fused_computation.22.clone.1 | loop fusion | flops 41943040 | bytes 12584960 | tf_op jit(solution)/shard_map/convert.5
  312.1 15.5 %fusion.83 = bf16[1024,8]{0,1:T(8,128)(2,1)S(1)} fusion(bf16[8,8192]{1,0:T(8,128)(2,1)S(1)} %copy-done.10, bf16[4096,512]{1,0:T(8,128)(2,1)} %get-tuple-element.209, bf16[4096,512]{1,0:T(8,128)(2,1)} %get-tuple-element.210, bf16[4096,512]{1,0:T(8,128)(2,1)} %get-tuple-element.211), kind=kOutput, calls=%fused_computation.29.clone.1 | convolution fusion | flops 201334784 | bytes 12730368 | tf_op jit(solution)/shard_map/while/body/eval_jaxpr/dot_general | solution.py:35
  329.1 37.2 %negate_convert_fusion.4 = (bf16[4096,512]{1,0:T(8,128)(2,1)}, bf16[4096,512]{1,0:T(8,128)(2,1)}, bf16[4096,512]{1,0:T(8,128)(2,1)}) fusion(s32[512]{0:T(512)S(1)} %iota_add_fusion.5), kind=kLoop, calls=%fused_computation.22.clone.1 | loop fusion | flops 41943040 | bytes 12584960 | tf_op jit(solution)/shard_map/convert.5
  366.3 15.5 %fusion.83 = bf16[1024,8]{0,1:T(8,128)(2,1)S(1)} fusion(bf16[8,8192]{1,0:T(8,128)(2,1)S(1)} %copy-done.10, bf16[4096,512]{1,0:T(8,128)(2,1)} %get-tuple-element.209, bf16[4096,512]{1,0:T(8,128)(2,1)} %get-tuple-element.210, bf16[4096,512]{1,0:T(8,128)(2,1)} %get-tuple-element.211), kind=kOutput, calls=%fused_computation.29.clone.1 | convolution fusion | flops 201334784 | bytes 12730368 | tf_op jit(solution)/shard_map/while/body/eval_jaxpr/dot_general | solution.py:35
  383.3 37.2 %negate_convert_fusion.4 = (bf16[4096,512]{1,0:T(8,128)(2,1)}, bf16[4096,512]{1,0:T(8,128)(2,1)}, bf16[4096,512]{1,0:T(8,128)(2,1)}) fusion(s32[512]{0:T(512)S(1)} %iota_add_fusion.5), kind=kLoop, calls=%fused_computation.22.clone.1 | loop fusion | flops 41943040 | bytes 12584960 | tf_op jit(solution)/shard_map/convert.5
  420.5 15.5 %fusion.83 = bf16[1024,8]{0,1:T(8,128)(2,1)S(1)} fusion(bf16[8,8192]{1,0:T(8,128)(2,1)S(1)} %copy-done.10, bf16[4096,512]{1,0:T(8,128)(2,1)} %get-tuple-element.209, bf16[4096,512]{1,0:T(8,128)(2,1)} %get-tuple-element.210, bf16[4096,512]{1,0:T(8,128)(2,1)} %get-tuple-element.211), kind=kOutput, calls=%fused_computation.29.clone.1 | convolution fusion | flops 201334784 | bytes 12730368 | tf_op jit(solution)/shard_map/while/body/eval_jaxpr/dot_general | solution.py:35
  439.3 29.9 %gather_fusion.1 = bf16[8192,8]{1,0:T(8,128)(2,1)} fusion(bf16[8,8192]{0,1:T(8,128)(2,1)} %bitcast.83, s32[8192]{0:T(1024)S(1)} %broadcast_clamp_fusion), kind=kCustom, calls=%fused_computation.1 | custom fusion | bytes 294912 | tf_op jit(solution)/shard_map/gather | solution.py:104
  469.2 29.8 %gather_fusion = bf16[8192,8]{1,0:T(8,128)(2,1)} fusion(bf16[8,8192]{0,1:T(8,128)(2,1)} %bitcast.84, s32[8192]{0:T(1024)S(1)} %broadcast_clamp_fusion.1), kind=kCustom, calls=%fused_computation | custom fusion | bytes 294912 | tf_op jit(solution)/shard_map/gather | solution.py:103
  504.2 12.5 scatter_fusion
  516.6 11.5 all-to-all-start
  532.5 2.2 fusion.72
  534.7 12.6 %all-to-all-done = bf16[128,4,8,128]{3,2,1,0:T(8,128)(2,1)S(1)} async-done(((bf16[128,4,8,128]{3,2,1,0:T(8,128)(2,1)}), bf16[128,4,8,128]{3,2,1,0:T(8,128)(2,1)S(1)}, u32[]{:S(2)}, u32[]{:S(2)}) %all-to-all-start) | async-done | bytes 1048608 | tf_op jit(solution)/shard_map/all_to_all | solution.py:63
  551.0 2.2 copy.42
  555.0 4.7 all-to-all-start.1
  560.1 18.9 %all-to-all-done.1 = bf16[128,4,8,128]{3,2,1,0:T(8,128)(2,1)S(1)} async-done(((bf16[128,4,8,128]{3,2,1,0:T(8,128)(2,1)}), bf16[128,4,8,128]{3,2,1,0:T(8,128)(2,1)S(1)}, u32[]{:S(2)}, u32[]{:S(2)}) %all-to-all-start.1) | async-done | bytes 1048608 | tf_op jit(solution)/shard_map/all_to_all | solution.py:67
  579.9 2.6 copy.52
  582.5 2.7 copy.51
  585.2 46.5 %scatter_custom_fusion.1 = f32[8,8192]{0,1:T(8,128)} fusion(s32[8192]{0:T(1024)S(1)} %reshape.296, f32[8192,8]{1,0:T(8,128)} %bitcast.87, f32[]{:T(128)} %constant.147.clone.1), kind=kCustom, calls=%fused_computation.64 | custom fusion | flops 65536 | bytes 262656
  631.7 44.0 %scatter_fusion.1 = f32[8,8192]{0,1:T(8,128)} fusion(f32[8,8192]{0,1:T(8,128)} %scatter_custom_fusion.1, s32[8192]{0:T(1024)S(1)} %reshape.302, f32[8192,8]{1,0:T(8,128)} %bitcast.86), kind=kCustom, calls=%fused_computation.7 | custom fusion | flops 65536 | bytes 819200
  675.7 2.4 convert_element_type.72
  678.9 577.7 %while.26 = (s32[]{:T(128)}, f32[8,8192]{1,0:T(8,128)S(1)}, bf16[8,2,8,512]{3,1,0,2:T(2,128)(2,1)S(1)}, s32[]{:T(128)}, s32[]{:T(128)}, /*index=5*/s32[]{:T(128)}) while((s32[]{:T(128)}, f32[8,8192]{1,0:T(8,128)S(1)}, bf16[8,2,8,512]{3,1,0,2:T(2,128)(2,1)S(1)}, s32[]{:T(128)}, s32[]{:T(128)}, /*index=5*/s32[]{:T(128)}) %tuple.74), condition=%wide.region_9.10_spmd.clone, body=%wide.region_8.9_spmd.clone.sunk | while | flops 243401216 | bytes 25776236 | solution.py:57
  679.0 35.7 %negate_convert_fusion.5 = (bf16[4096,512]{1,0:T(8,128)(2,1)S(1)}, bf16[4096,512]{1,0:T(8,128)(2,1)S(1)}, bf16[4096,512]{1,0:T(8,128)(2,1)}) fusion(s32[512]{0:T(512)S(1)} %iota_add_fusion.6), kind=kLoop, calls=%fused_computation.48.clone.1 | loop fusion | flops 41943040 | bytes 12584960 | tf_op jit(solution)/shard_map/convert.11
  714.6 36.5 %fusion.86 = f32[8,8192]{1,0:T(8,128)S(1)} fusion(bf16[8,1024]{1,0:T(8,128)(2,1)S(1)} %bitcast.93, bf16[4096,512]{1,0:T(8,128)(2,1)} %get-tuple-element.215, bf16[4096,512]{1,0:T(8,128)(2,1)S(1)} %get-tuple-element.216, bf16[4096,512]{1,0:T(8,128)(2,1)S(1)} %get-tuple-element.217, f32[8,8192]{1,0:T(8,128)S(1)} %get-tuple-element.243, pred[]{:T(512)S(6)} %compare.40), kind=kOutput, calls=%fused_computation.44.clone.1 | convolution fusion | flops 201457664 | bytes 13123585 | tf_op jit(solution)/shard_map/while/body/dot_general | solution.py:53
  751.2 35.7 %negate_convert_fusion.5 = (bf16[4096,512]{1,0:T(8,128)(2,1)S(1)}, bf16[4096,512]{1,0:T(8,128)(2,1)S(1)}, bf16[4096,512]{1,0:T(8,128)(2,1)}) fusion(s32[512]{0:T(512)S(1)} %iota_add_fusion.6), kind=kLoop, calls=%fused_computation.48.clone.1 | loop fusion | flops 41943040 | bytes 12584960 | tf_op jit(solution)/shard_map/convert.11
  786.8 36.5 %fusion.86 = f32[8,8192]{1,0:T(8,128)S(1)} fusion(bf16[8,1024]{1,0:T(8,128)(2,1)S(1)} %bitcast.93, bf16[4096,512]{1,0:T(8,128)(2,1)} %get-tuple-element.215, bf16[4096,512]{1,0:T(8,128)(2,1)S(1)} %get-tuple-element.216, bf16[4096,512]{1,0:T(8,128)(2,1)S(1)} %get-tuple-element.217, f32[8,8192]{1,0:T(8,128)S(1)} %get-tuple-element.243, pred[]{:T(512)S(6)} %compare.40), kind=kOutput, calls=%fused_computation.44.clone.1 | convolution fusion | flops 201457664 | bytes 13123585 | tf_op jit(solution)/shard_map/while/body/dot_general | solution.py:53
  823.4 35.7 %negate_convert_fusion.5 = (bf16[4096,512]{1,0:T(8,128)(2,1)S(1)}, bf16[4096,512]{1,0:T(8,128)(2,1)S(1)}, bf16[4096,512]{1,0:T(8,128)(2,1)}) fusion(s32[512]{0:T(512)S(1)} %iota_add_fusion.6), kind=kLoop, calls=%fused_computation.48.clone.1 | loop fusion | flops 41943040 | bytes 12584960 | tf_op jit(solution)/shard_map/convert.11
  859.0 36.5 %fusion.86 = f32[8,8192]{1,0:T(8,128)S(1)} fusion(bf16[8,1024]{1,0:T(8,128)(2,1)S(1)} %bitcast.93, bf16[4096,512]{1,0:T(8,128)(2,1)} %get-tuple-element.215, bf16[4096,512]{1,0:T(8,128)(2,1)S(1)} %get-tuple-element.216, bf16[4096,512]{1,0:T(8,128)(2,1)S(1)} %get-tuple-element.217, f32[8,8192]{1,0:T(8,128)S(1)} %get-tuple-element.243, pred[]{:T(512)S(6)} %compare.40), kind=kOutput, calls=%fused_computation.44.clone.1 | convolution fusion | flops 201457664 | bytes 13123585 | tf_op jit(solution)/shard_map/while/body/dot_general | solution.py:53
  895.6 35.7 %negate_convert_fusion.5 = (bf16[4096,512]{1,0:T(8,128)(2,1)S(1)}, bf16[4096,512]{1,0:T(8,128)(2,1)S(1)}, bf16[4096,512]{1,0:T(8,128)(2,1)}) fusion(s32[512]{0:T(512)S(1)} %iota_add_fusion.6), kind=kLoop, calls=%fused_computation.48.clone.1 | loop fusion | flops 41943040 | bytes 12584960 | tf_op jit(solution)/shard_map/convert.11
  931.2 36.5 %fusion.86 = f32[8,8192]{1,0:T(8,128)S(1)} fusion(bf16[8,1024]{1,0:T(8,128)(2,1)S(1)} %bitcast.93, bf16[4096,512]{1,0:T(8,128)(2,1)} %get-tuple-element.215, bf16[4096,512]{1,0:T(8,128)(2,1)S(1)} %get-tuple-element.216, bf16[4096,512]{1,0:T(8,128)(2,1)S(1)} %get-tuple-element.217, f32[8,8192]{1,0:T(8,128)S(1)} %get-tuple-element.243, pred[]{:T(512)S(6)} %compare.40), kind=kOutput, calls=%fused_computation.44.clone.1 | convolution fusion | flops 201457664 | bytes 13123585 | tf_op jit(solution)/shard_map/while/body/dot_general | solution.py:53
  967.8 35.7 %negate_convert_fusion.5 = (bf16[4096,512]{1,0:T(8,128)(2,1)S(1)}, bf16[4096,512]{1,0:T(8,128)(2,1)S(1)}, bf16[4096,512]{1,0:T(8,128)(2,1)}) fusion(s32[512]{0:T(512)S(1)} %iota_add_fusion.6), kind=kLoop, calls=%fused_computation.48.clone.1 | loop fusion | flops 41943040 | bytes 12584960 | tf_op jit(solution)/shard_map/convert.11
  1003.4 36.5 %fusion.86 = f32[8,8192]{1,0:T(8,128)S(1)} fusion(bf16[8,1024]{1,0:T(8,128)(2,1)S(1)} %bitcast.93, bf16[4096,512]{1,0:T(8,128)(2,1)} %get-tuple-element.215, bf16[4096,512]{1,0:T(8,128)(2,1)S(1)} %get-tuple-element.216, bf16[4096,512]{1,0:T(8,128)(2,1)S(1)} %get-tuple-element.217, f32[8,8192]{1,0:T(8,128)S(1)} %get-tuple-element.243, pred[]{:T(512)S(6)} %compare.40), kind=kOutput, calls=%fused_computation.44.clone.1 | convolution fusion | flops 201457664 | bytes 13123585 | tf_op jit(solution)/shard_map/while/body/dot_general | solution.py:53
  1040.0 35.7 %negate_convert_fusion.5 = (bf16[4096,512]{1,0:T(8,128)(2,1)S(1)}, bf16[4096,512]{1,0:T(8,128)(2,1)S(1)}, bf16[4096,512]{1,0:T(8,128)(2,1)}) fusion(s32[512]{0:T(512)S(1)} %iota_add_fusion.6), kind=kLoop, calls=%fused_computation.48.clone.1 | loop fusion | flops 41943040 | bytes 12584960 | tf_op jit(solution)/shard_map/convert.11
  1075.7 36.5 %fusion.86 = f32[8,8192]{1,0:T(8,128)S(1)} fusion(bf16[8,1024]{1,0:T(8,128)(2,1)S(1)} %bitcast.93, bf16[4096,512]{1,0:T(8,128)(2,1)} %get-tuple-element.215, bf16[4096,512]{1,0:T(8,128)(2,1)S(1)} %get-tuple-element.216, bf16[4096,512]{1,0:T(8,128)(2,1)S(1)} %get-tuple-element.217, f32[8,8192]{1,0:T(8,128)S(1)} %get-tuple-element.243, pred[]{:T(512)S(6)} %compare.40), kind=kOutput, calls=%fused_computation.44.clone.1 | convolution fusion | flops 201457664 | bytes 13123585 | tf_op jit(solution)/shard_map/while/body/dot_general | solution.py:53
  1112.2 35.7 %negate_convert_fusion.5 = (bf16[4096,512]{1,0:T(8,128)(2,1)S(1)}, bf16[4096,512]{1,0:T(8,128)(2,1)S(1)}, bf16[4096,512]{1,0:T(8,128)(2,1)}) fusion(s32[512]{0:T(512)S(1)} %iota_add_fusion.6), kind=kLoop, calls=%fused_computation.48.clone.1 | loop fusion | flops 41943040 | bytes 12584960 | tf_op jit(solution)/shard_map/convert.11
  1147.9 36.5 %fusion.86 = f32[8,8192]{1,0:T(8,128)S(1)} fusion(bf16[8,1024]{1,0:T(8,128)(2,1)S(1)} %bitcast.93, bf16[4096,512]{1,0:T(8,128)(2,1)} %get-tuple-element.215, bf16[4096,512]{1,0:T(8,128)(2,1)S(1)} %get-tuple-element.216, bf16[4096,512]{1,0:T(8,128)(2,1)S(1)} %get-tuple-element.217, f32[8,8192]{1,0:T(8,128)S(1)} %get-tuple-element.243, pred[]{:T(512)S(6)} %compare.40), kind=kOutput, calls=%fused_computation.44.clone.1 | convolution fusion | flops 201457664 | bytes 13123585 | tf_op jit(solution)/shard_map/while/body/dot_general | solution.py:53
  1184.4 35.7 %negate_convert_fusion.5 = (bf16[4096,512]{1,0:T(8,128)(2,1)S(1)}, bf16[4096,512]{1,0:T(8,128)(2,1)S(1)}, bf16[4096,512]{1,0:T(8,128)(2,1)}) fusion(s32[512]{0:T(512)S(1)} %iota_add_fusion.6), kind=kLoop, calls=%fused_computation.48.clone.1 | loop fusion | flops 41943040 | bytes 12584960 | tf_op jit(solution)/shard_map/convert.11
  1220.1 36.5 %fusion.86 = f32[8,8192]{1,0:T(8,128)S(1)} fusion(bf16[8,1024]{1,0:T(8,128)(2,1)S(1)} %bitcast.93, bf16[4096,512]{1,0:T(8,128)(2,1)} %get-tuple-element.215, bf16[4096,512]{1,0:T(8,128)(2,1)S(1)} %get-tuple-element.216, bf16[4096,512]{1,0:T(8,128)(2,1)S(1)} %get-tuple-element.217, f32[8,8192]{1,0:T(8,128)S(1)} %get-tuple-element.243, pred[]{:T(512)S(6)} %compare.40), kind=kOutput, calls=%fused_computation.44.clone.1 | convolution fusion | flops 201457664 | bytes 13123585 | tf_op jit(solution)/shard_map/while/body/dot_general | solution.py:53
  (132 shorter events, 30.2 us)
Async XLA Ops:
  0.0 528.9 %copy-start = (bf16[16,64,1024]{2,1,0:T(8,128)(2,1)S(1)}, bf16[16,64,1024]{2,1,0:T(8,128)(2,1)}, u32[]{:S(2)}) copy-start(bf16[16,64,1024]{2,1,0:T(8,128)(2,1)} %param.16) | copy-start | bytes 6291460
  2.6 433.5 %copy-start.9 = (s32[16]{0:T(128)S(1)}, s32[16]{0:T(128)}, u32[]{:S(2)}) copy-start(s32[16]{0:T(128)} %param.12) | copy-start | bytes 196
  2.6 434.1 %copy-start.11 = (s32[128]{0:T(128)S(1)}, s32[128]{0:T(128)}, u32[]{:S(2)}) copy-start(s32[128]{0:T(128)} %param.13) | copy-start | bytes 1540
  4.0 37.2 %copy-start.10 = (bf16[8,8192]{1,0:T(8,128)(2,1)S(1)}, bf16[8,8192]{1,0:T(8,128)(2,1)}, u32[]{:S(2)}) copy-start(bf16[8,8192]{1,0:T(8,128)(2,1)} %get-tuple-element.233) | copy-start | bytes 393220 | tf_op jit(solution)/shard_map/while
  58.1 37.2 %copy-start.10 = (bf16[8,8192]{1,0:T(8,128)(2,1)S(1)}, bf16[8,8192]{1,0:T(8,128)(2,1)}, u32[]{:S(2)}) copy-start(bf16[8,8192]{1,0:T(8,128)(2,1)} %get-tuple-element.233) | copy-start | bytes 393220 | tf_op jit(solution)/shard_map/while
  112.3 37.2 %copy-start.10 = (bf16[8,8192]{1,0:T(8,128)(2,1)S(1)}, bf16[8,8192]{1,0:T(8,128)(2,1)}, u32[]{:S(2)}) copy-start(bf16[8,8192]{1,0:T(8,128)(2,1)} %get-tuple-element.233) | copy-start | bytes 393220 | tf_op jit(solution)/shard_map/while
  166.5 37.2 %copy-start.10 = (bf16[8,8192]{1,0:T(8,128)(2,1)S(1)}, bf16[8,8192]{1,0:T(8,128)(2,1)}, u32[]{:S(2)}) copy-start(bf16[8,8192]{1,0:T(8,128)(2,1)} %get-tuple-element.233) | copy-start | bytes 393220 | tf_op jit(solution)/shard_map/while
  220.7 37.2 %copy-start.10 = (bf16[8,8192]{1,0:T(8,128)(2,1)S(1)}, bf16[8,8192]{1,0:T(8,128)(2,1)}, u32[]{:S(2)}) copy-start(bf16[8,8192]{1,0:T(8,128)(2,1)} %get-tuple-element.233) | copy-start | bytes 393220 | tf_op jit(solution)/shard_map/while
  274.9 37.2 %copy-start.10 = (bf16[8,8192]{1,0:T(8,128)(2,1)S(1)}, bf16[8,8192]{1,0:T(8,128)(2,1)}, u32[]{:S(2)}) copy-start(bf16[8,8192]{1,0:T(8,128)(2,1)} %get-tuple-element.233) | copy-start | bytes 393220 | tf_op jit(solution)/shard_map/while
  329.1 37.2 %copy-start.10 = (bf16[8,8192]{1,0:T(8,128)(2,1)S(1)}, bf16[8,8192]{1,0:T(8,128)(2,1)}, u32[]{:S(2)}) copy-start(bf16[8,8192]{1,0:T(8,128)(2,1)} %get-tuple-element.233) | copy-start | bytes 393220 | tf_op jit(solution)/shard_map/while
  383.2 37.2 %copy-start.10 = (bf16[8,8192]{1,0:T(8,128)(2,1)S(1)}, bf16[8,8192]{1,0:T(8,128)(2,1)}, u32[]{:S(2)}) copy-start(bf16[8,8192]{1,0:T(8,128)(2,1)} %get-tuple-element.233) | copy-start | bytes 393220 | tf_op jit(solution)/shard_map/while
  499.0 29.1 %copy-start.6 = (s32[128]{0:T(128)S(1)}, s32[128]{0:T(128)}, u32[]{:S(2)}) copy-start(s32[128]{0:T(128)} %param.14) | copy-start | bytes 1540
  499.0 29.3 %copy-start.2 = (s32[128]{0:T(128)S(1)}, s32[128]{0:T(128)}, u32[]{:S(2)}) copy-start(s32[128]{0:T(128)} %param.15) | copy-start | bytes 1540
  516.6 30.7 %all-to-all-start = ((bf16[128,4,8,128]{3,2,1,0:T(8,128)(2,1)}), bf16[128,4,8,128]{3,2,1,0:T(8,128)(2,1)S(1)}, u32[]{:S(2)}, u32[]{:S(2)}) async-start(bf16[128,4,8,128]{3,2,1,0:T(8,128)(2,1)} %bitcast.15), calls=%async_computation | async-start | bytes 2097152 | tf_op jit(solution)/shard_map/all_to_all | solution.py:63
  548.1 1.1 copy-start.3
  548.1 1.2 copy-start.4
  548.1 1.2 copy-start.5
  551.0 8.7 copy-start.8
  551.0 8.8 copy-start.7
  555.0 24.0 %all-to-all-start.1 = ((bf16[128,4,8,128]{3,2,1,0:T(8,128)(2,1)}), bf16[128,4,8,128]{3,2,1,0:T(8,128)(2,1)S(1)}, u32[]{:S(2)}, u32[]{:S(2)}) async-start(bf16[128,4,8,128]{3,2,1,0:T(8,128)(2,1)} %reshape.234), calls=%async_computation.1 | async-start | bytes 2097152 | tf_op jit(solution)/shard_map/all_to_all | solution.py:67
  1256.6 0.7 copy-start.12
  1256.6 1.7 copy-start.1
where the time goes:
time: 1260 us
  other arithmetic  680 us (54%)
  matrix products  418 us (33%)
  local copies, waits for them, and re-layouts  105 us (8%)
  waiting for transfers between devices  31.5 us (2%)
  starting transfers between devices  16.1 us (1%)
    another operation x17, other arithmetic  583 us
    dot_general x8, matrix products, add_block(): lax.dot_general(piece, block, (((1,), (1,)), ((), ())), preferred_element...  292 us
    dot_general x8, matrix products, one_block(): product = jnp.dot(rows, block, preferred_element_type=jnp.float32)  124 us
    unnamed x6, other arithmetic  90.7 us
    gather x2, local copies, waits for them, and re-layouts, local(): imag_part = spectrum[:, FL + chosen_freq]  31.8 us
    gather x2, local copies, waits for them, and re-layouts, local(): real_part = spectrum[:, chosen_freq]  31.8 us
  transfers between devices with their start and end apart: 2, of which 2 were waited for; matrix products, arithmetic and copies ran while one was open for 1% of the time, Pallas kernels for 0%

commit v1 on v0

v1 whole, which is shorter than its diff:
```python
import functools
import math

import jax
import jax.numpy as jnp
import numpy as np
from jax import lax
from jax.experimental import pallas as pl
from jax.experimental.pallas import tpu as pltpu
from jax.sharding import PartitionSpec as P

FL = 4096
CAP = 4
NF = 16
NS = 8
ROWS = 8
MINE = 8
BLOCKS = 9
MESH = pl.DeviceIdType.MESH
F32 = jnp.float32
BF16 = jnp.bfloat16


def split_halves(table):
    high = table.astype(np.float32).astype(jnp.bfloat16)
    low = (table - high.astype(np.float64)).astype(np.float32).astype(jnp.bfloat16)
    return high, low


def make_tables():
    k = np.arange(64)
    u = np.arange(32)
    b = np.arange(128)
    tau = 2.0 * np.pi
    first = tau * ((2 * k[:, None] * u[None, :]) % 64) / 64
    twist = tau * ((k[:, None] * b[None, :]) % FL) / FL
    last = tau * ((k[:, None] * b[None, :]) % 64) / 64
    scale = 1.0 / math.sqrt(FL)
    c, s = np.cos(first) * scale, np.sin(first) * scale
    ahead = np.block([[c, s], [-s, c]])
    back = np.block([[c.T, -s.T], [s.T, c.T]])
    forward_rows = np.zeros((128, 256))
    forward_rows[:64, :128] = np.cos(last)
    forward_rows[:64, 128:] = np.sin(last)
    backward_rows = np.zeros((128, 128))
    backward_rows[:64, :64] = np.cos(last[:, :64]).T
    backward_rows[64:, :64] = np.sin(last[:, :64]).T
    ct, st = np.cos(twist), np.sin(twist)
    twist_ahead = np.stack([ct, st]).astype(np.float32)
    twist_back = np.stack([np.concatenate([ct.T, ct.T], 1), np.concatenate([-st.T, st.T], 1)]).astype(np.float32)
    return (
        np.stack(split_halves(ahead)),
        twist_ahead,
        np.stack(split_halves(forward_rows)),
        np.stack(split_halves(backward_rows)),
        twist_back,
        np.stack(split_halves(back)),
    )


def mm(a, b):
    return jnp.dot(a, b, preferred_element_type=F32)


def mm_nt(a, b):
    return lax.dot_general(a, b, (((1,), (1,)), ((), ())), preferred_element_type=F32)


def halves(x):
    high = x.astype(BF16)
    return high, (x - high.astype(F32)).astype(BF16)


def iota(shape, dim):
    return lax.broadcasted_iota(jnp.int32, shape, dim)


def kernel(
    fo, so, si, so_v, ow_v, strips, gw, ahead, twa, frow, brow, twb, back, screens, out,
    xs, col, qsc, wblk, bsc, scr, sbuf, rbuf, esend, ebuf, wmsg, wrows, wpart, wall, oscr,
    scr_sem, s1, r1, s2, r2, sw1, rw1, sw2, rw2,
):
    f = lax.axis_index("facet")
    s = lax.axis_index("sub")
    fx, fy = f // 4, f % 4
    steps = [(dx, dy) for dx in range(4) for dy in range(4) if (dx, dy) != (0, 0)]
    steps.sort(key=lambda d: -(min(d[0], 4 - d[0]) + min(d[1], 4 - d[1])))
    peers = [((fx + dx) % 4) * 4 + (fy + dy) % 4 for dx, dy in steps]
    senders = [((fx - dx + 4) % 4) * 4 + (fy - dy + 4) % 4 for dx, dy in steps]

    barrier = pltpu.get_barrier_semaphore()
    for p in peers:
        pl.semaphore_signal(barrier, inc=1, device_id=(p, s), device_id_type=MESH)
    for d in range(1, NS):
        pl.semaphore_signal(barrier, inc=1, device_id=(f, (s + d) % NS), device_id_type=MESH)

    screen_copy = pltpu.make_async_copy(screens.at[:, pl.ds(pl.multiple_of(s * ROWS, ROWS), ROWS), :], scr, scr_sem)
    screen_copy.start()

    for q in range(4):
        wmsg[pl.ds(4 * q, 4), :] = gw[:, 128 * q : 128 * q + 128]
    wrows[pl.ds(f, 1)] = wmsg[...].astype(BF16)[None]

    lane = iota((128, 128), 1)
    sub_i = iota((128, 128), 0)
    low6 = lane & 63
    so_row = jnp.broadcast_to(so_v[...], (128, 128))
    ow_row = jnp.broadcast_to(ow_v[...], (128, 128))
    so_col = jnp.transpose(so_row)
    ow_col = jnp.transpose(ow_row)
    earlier = jnp.where((ow_row == ow_col) & (lane < sub_i), 1.0, 0.0)
    slot = jnp.sum(earlier, axis=1, keepdims=True).astype(jnp.int32)
    col[0] = so_col
    col[1] = ow_col * CAP + slot

    my_offset = fo[f]
    start_col = (so_col + my_offset) & (FL - 1)
    q_col = start_col >> 6
    take_low = low6 >= (start_col & 63)
    start_row = (so_row + my_offset) & (FL - 1)
    q_row = start_row >> 6

    pick = jnp.concatenate(
        [jnp.where(lane == q_col, 1.0, 0.0), jnp.where(lane == ((q_col + 1) & 63), 1.0, 0.0)], axis=0
    ).astype(BF16)
    tf_high = mm(pick, frow[0]).astype(BF16)
    tf_low = mm(pick, frow[1]).astype(BF16)
    for v in range(64):
        xs[pl.ds(8 * v, 8), :] = strips[:, 128 * v : 128 * v + 128].astype(F32)
    tc, ts = twa[0], twa[1]

    def contributions(row):
        x = xs[pl.ds(row, 64, stride=8), :].astype(BF16)
        a = mm(ahead[0], x) + mm(ahead[1], x)
        re, im = a[:64], a[64:]
        b_re = re * tc + im * ts
        b_im = im * tc - re * ts
        b = jnp.concatenate(
            [jnp.concatenate([b_re, b_im], axis=1), jnp.concatenate([b_im, -b_re], axis=1)], axis=0
        )
        b_high, b_low = halves(b)
        g = mm_nt(tf_high, b_high) + mm_nt(tf_low, b_high) + mm_nt(tf_high, b_low)
        return jnp.where(take_low, g[:128], g[128:])

    for pair in range(ROWS // 2):
        c0 = contributions(2 * pair).reshape(NF, MINE, 128)
        c1 = contributions(2 * pair + 1).reshape(NF, MINE, 128)
        both = jnp.concatenate([c0, c1], axis=1).astype(BF16)
        sbuf[:, pair] = both
    rbuf[pl.ds(f, 1)] = sbuf[pl.ds(f, 1)]

    pl.semaphore_wait(barrier, NF - 1 + NS - 1)

    def remote(src, dst, send, recv, to):
        return pltpu.make_async_remote_copy(
            src_ref=src, dst_ref=dst, send_sem=send, recv_sem=recv, device_id=to, device_id_type=MESH
        )

    w1 = [remote(wrows.at[f], wrows.at[f], sw1.at[n], rw1.at[n], (p, s)) for n, p in enumerate(peers)]
    a1 = [remote(sbuf.at[p], rbuf.at[f], s1.at[n], r1.at[n], (p, s)) for n, p in enumerate(peers)]
    for c in w1:
        c.start()
    for c in a1:
        c.start()

    pick_t = jnp.concatenate(
        [jnp.where(sub_i == q_row, 1.0, 0.0), jnp.where(sub_i == ((q_row + 1) & 63), 1.0, 0.0)], axis=1
    ).astype(BF16)
    tb_high = mm(brow[0], pick_t).astype(BF16)
    tb_low = mm(brow[1], pick_t).astype(BF16)

    lane8 = iota((8, 128), 1)
    left = lane8 < 64
    base = pl.multiple_of(f * MINE, MINE)
    so8 = col[0, pl.ds(base, MINE), :]
    wr8 = col[1, pl.ds(base, MINE), :]
    r8 = so8 & 63
    zero = jnp.zeros((8, 128), F32)
    screen_copy.wait()

    def to_blocks(pieces):
        blocks = []
        for piece in pieces:
            other = pltpu.roll(piece, 64, 1)
            blocks.append(jnp.where(left, piece, other))
            blocks.append(jnp.where(left, other, piece))
        return blocks[:BLOCKS]

    for j in range(MINE):
        shift = so[base + j] & 63
        screen = scr[si[base + j]].astype(F32)
        for part in range(2):
            rolled = [
                pltpu.roll(screen[:, 512 * part + 128 * v : 512 * part + 128 * v + 128], shift, 1) for v in range(4)
            ]
            rolled = [zero] + rolled + [zero]
            pieces = [jnp.where(lane8 >= shift, rolled[v + 1], rolled[v]) for v in range(5)]
            for n, block in enumerate(to_blocks(pieces)):
                value = jnp.where(left, -block, block) if part else block
                qsc[part, n, pl.ds(j, ROWS, stride=MINE), :] = value

    for n in range(NF):
        start = r8 + fo[n]
        bsc[n] = (start >> 6) + jnp.where((lane8 & 63) < (start & 63), 1, 0)

    for n, p in enumerate(senders):
        remote(wrows.at[f], wrows.at[p], sw1.at[n], rw1.at[n], (p, s)).wait_recv()
    lane256 = iota((8, 256), 1)
    target = (lane256 >> 4) * (NS * CAP) + s * CAP + (lane256 & 3)
    wanted = jnp.concatenate([wr8, wr8], axis=1) == target
    chosen = jnp.concatenate(
        [jnp.where(wanted & (((lane256 >> 2) & 3) == q), 1.0, 0.0) for q in range(4)], axis=0
    ).astype(BF16)
    part_rows = mm(chosen, wrows[...].reshape(256, 128)).astype(BF16)
    wpart[...] = part_rows
    wall[pl.ds(s, 1)] = part_rows[None]
    w2 = [
        remote(wpart, wall.at[s], sw2.at[d - 1], rw2.at[d - 1], (f, (s + d) % NS)) for d in range(1, NS)
    ]
    for c in w2:
        c.start()
    for d in range(1, NS):
        p = (s - d + NS) % NS
        remote(wpart, wall.at[p], sw2.at[d - 1], rw2.at[d - 1], (f, p)).wait_recv()
    w32 = wall[0].astype(F32)
    for p in range(1, NS):
        w32 = w32 + wall[p].astype(F32)
    pieces = [w32[8 * q : 8 * q + 8] for q in range(4)] + [zero]
    for bit in range(6):
        amount = 1 << bit
        turned = [zero] + [pltpu.roll(piece, amount, 1) for piece in pieces]
        moved = [jnp.where(lane8 >= amount, turned[v + 1], turned[v]) for v in range(5)]
        on = (r8 & amount) != 0
        pieces = [jnp.where(on, moved[v], pieces[v]) for v in range(5)]
    for n, block in enumerate(to_blocks(pieces)):
        wblk[n] = block

    for n, p in enumerate(senders):
        remote(sbuf.at[p], rbuf.at[p], s1.at[n], r1.at[n], (p, s)).wait_recv()

    def process(pair, carry):
        got = [rbuf[n, pair].astype(F32) for n in range(NF)]
        sent = []
        for half in range(2):
            row = 2 * pair + half
            sums = [zero] * BLOCKS
            for n in range(NF):
                piece = got[n][8 * half : 8 * half + 8]
                where = bsc[n]
                for b in range(BLOCKS):
                    sums[b] = sums[b] + jnp.where(where == b, piece, 0.0)
            done = []
            at = pl.ds(pl.multiple_of(row * MINE, MINE), MINE)
            for b in range(BLOCKS):
                turned = pltpu.roll(sums[b], 64, 1)
                done.append((sums[b] * qsc[0, b, at, :] + turned * qsc[1, b, at, :]) * wblk[b])
            picked = []
            for n in range(NF):
                where = bsc[n]
                piece = done[0]
                for b in range(1, BLOCKS):
                    piece = jnp.where(where == b, done[b], piece)
                picked.append(piece)
            sent.append(picked)
        for n in range(NF):
            esend[n, pair] = jnp.concatenate([sent[0][n], sent[1][n]], axis=0).astype(BF16)
        return carry

    lax.fori_loop(0, ROWS // 2, process, 0)

    ebuf[pl.ds(f, 1)] = esend[pl.ds(f, 1)]
    a2 = [remote(esend.at[p], ebuf.at[f], s2.at[n], r2.at[n], (p, s)) for n, p in enumerate(peers)]
    for c in a2:
        c.start()
    for c in w1 + a1 + w2:
        c.wait_send()
    for n, p in enumerate(senders):
        remote(esend.at[p], ebuf.at[p], s2.at[n], r2.at[n], (p, s)).wait_recv()

    bc, bs = twb[0], twb[1]
    sign = jnp.where(iota((64, 128), 1) < 64, -1.0, 1.0)
    for row in range(ROWS):
        e = ebuf[:, row // 2].astype(F32)[:, 8 * (row % 2) : 8 * (row % 2) + 8].reshape(128, 128)
        e2 = jnp.concatenate([jnp.where(take_low, e, 0.0), jnp.where(take_low, 0.0, e)], axis=0).astype(BF16)
        both = mm(tb_high, e2) + mm(tb_low, e2)
        d = both[:64] + sign * pltpu.roll(both[64:], 64, 1)
        turned = pltpu.roll(d, 64, 1)
        d2 = jnp.concatenate([d, d], axis=0) * bc + jnp.concatenate([turned, turned], axis=0) * bs
        d_high, d_low = halves(d2)
        o = mm_nt(back[0], d_high) + mm_nt(back[1], d_high) + mm_nt(back[0], d_low)
        oscr[pl.ds(row, 64, stride=8), :] = o
    for v in range(64):
        out[:, 128 * v : 128 * v + 128] = oscr[pl.ds(8 * v, 8), :]
    for c in a2:
        c.wait_send()


def local(strips, facet_offset, subgrid_offset, owner, screen_index, screens, grid_weight):
    tables = [jnp.asarray(t) for t in make_tables()]
    vmem = pl.BlockSpec(memory_space=pltpu.VMEM)
    smem = pl.BlockSpec(memory_space=pltpu.SMEM)
    result = pl.pallas_call(
        kernel,
        out_shape=jax.ShapeDtypeStruct((ROWS, 2 * FL), F32),
        in_specs=[smem] * 3 + [vmem] * 10 + [pl.BlockSpec(memory_space=pl.ANY)],
        out_specs=vmem,
        scratch_shapes=[
            pltpu.VMEM((576, 128), F32),
            pltpu.VMEM((2, 128, 128), jnp.int32),
            pltpu.VMEM((2, BLOCKS, 128, 128), F32),
            pltpu.VMEM((BLOCKS, 8, 128), F32),
            pltpu.VMEM((NF, 8, 128), jnp.int32),
            pltpu.VMEM((16, ROWS, 1024), BF16),
            pltpu.VMEM((NF, 4, 16, 128), BF16),
            pltpu.VMEM((NF, 4, 16, 128), BF16),
            pltpu.VMEM((NF, 4, 16, 128), BF16),
            pltpu.VMEM((NF, 4, 16, 128), BF16),
            pltpu.VMEM((16, 128), F32),
            pltpu.VMEM((NF, 16, 128), BF16),
            pltpu.VMEM((32, 128), BF16),
            pltpu.VMEM((NS, 32, 128), BF16),
            pltpu.VMEM((576, 128), F32),
            pltpu.SemaphoreType.DMA,
            pltpu.SemaphoreType.DMA((NF - 1,)),
            pltpu.SemaphoreType.DMA((NF - 1,)),
            pltpu.SemaphoreType.DMA((NF - 1,)),
            pltpu.SemaphoreType.DMA((NF - 1,)),
            pltpu.SemaphoreType.DMA((NF - 1,)),
            pltpu.SemaphoreType.DMA((NF - 1,)),
            pltpu.SemaphoreType.DMA((NS - 1,)),
            pltpu.SemaphoreType.DMA((NS - 1,)),
        ],
        compiler_params=pltpu.CompilerParams(collective_id=0, has_side_effects=True),
        name="round_trip",
    )(
        facet_offset,
        subgrid_offset,
        screen_index,
        subgrid_offset.reshape(1, -1),
        owner.reshape(1, -1),
        strips[0],
        grid_weight,
        *tables,
        screens,
    )
    return result[None]


def solution(mesh):
    in_specs = (P("facet", "sub", None), P(), P(), P(), P(), P(), P(("facet", "sub"), None))
    out_specs = P("facet", "sub", None)
    return jax.shard_map(local, mesh=mesh, in_specs=in_specs, out_specs=out_specs, check_vma=False)
```

time: 1260 us -> 30.4 us (0.02)
  other arithmetic: 680 us -> 0 us
  matrix products: 418 us -> 0 us
  local copies, waits for them, and re-layouts: 105 us -> 1.67 us
  waiting for transfers between devices: 31.5 us -> 0 us
  Pallas kernels: 0 us -> 28.6 us
  starting transfers between devices: 16.1 us -> 0 us
    another operation x18 -> x0, other arithmetic: 583 us -> none
    dot_general x18 -> x0, matrix products: 418 us -> none  [the longest x8 292 us: add_block(): lax.dot_general(piece, block, (((1,), (1,)), ((), ())), preferred_element...]
    unnamed x6 -> x0, other arithmetic: 90.7 us -> none
    gather x7 -> x0, local copies, waits for them, and re-layouts: 66.3 us -> none  [the longest x2 31.8 us: local(): imag_part = spectrum[:, FL + chosen_freq]]
    all_to_all x2 -> x0, waiting for transfers between devices: 31.5 us -> none  [the longest x1 18.9 us: send_back(): lax.all_to_all(buffer, ('facet', 'sub'), split_axis=0, concat_axis=0, til...]
    pallas_call x0 -> x1, Pallas kernels: none -> 28.6 us  [local(): pl.pallas_call(kernel, out_shape=jax.ShapeDtypeStruct((ROWS, 2 * FL), F32...]
    all_to_all x2 -> x0, starting transfers between devices: 16.1 us -> none  [the longest x1 11.5 us: send_forward(): lax.all_to_all(buffer, ('facet', 'sub'), split_axis=0, concat_axis=0, til...]
  transfers between devices with their start and end apart: 2 -> 0, of which waited for: 2 -> 0; matrix products, arithmetic and copies ran while one was open for 1% -> 0% of each run, Pallas kernels for 0% -> 0%
where the time goes in v1:
time: 30.4 us; the launch traced here: 30.3 us
  Pallas kernels  28.6 us (94%)
  local copies, waits for them, and re-layouts  1.67 us (5%)
    pallas_call x1, Pallas kernels, local(): pl.pallas_call(kernel, out_shape=jax.ShapeDtypeStruct((ROWS, 2 * FL), F32...  28.6 us
    unnamed x1, local copies, waits for them, and re-layouts  1.67 us

profile of v1, /device:TPU:1, one launch (start us, length us, event | category | flops | bytes accessed | tf_op | source)
XLA Modules:
  0.0 30.3 jit_solution(9750299041412240057)
XLA Ops:
  0.0 28.6 %round_trip.1 = f32[8,8192]{1,0:T(8,128)} custom-call(s32[16]{0:T(128)} %fo.1, s32[128]{0:T(128)} %so.1, s32[128]{0:T(128)} %si.1, s32[1,128]{1,0:T(1,128)} %bitcast.6, s32[1,128]{1,0:T(1,128)} %bitcast.7, bf16[8,8192]{1,0:T(8,128)(2,1)} %bitcast.5, f32[4,512]{1,0:T(4,128)} %gw.1, bf16[2,128,64]{2,1,0:T(8,128)(2,1)} %constant.12.clone.ahead, ...), custom_call_target="tpu_custom_call" | custom-call | tf_op jit(solution)/shard_map/round_trip/pallas_call | solution.py:302
  28.6 1.7 %copy.15 = f32[1,8,8192]{2,1,0:T(8,128)} copy(f32[1,8,8192]{2,1,0:T(8,128)} %bitcast.4) | data formatting | bytes 524288

commit v2 on v0

v2 whole, which is shorter than its diff:
```python
import math

import jax
import jax.numpy as jnp
import numpy as np
from jax import lax
from jax.experimental import pallas as pl
from jax.experimental.pallas import tpu as pltpu
from jax.sharding import PartitionSpec as P

FL = 4096
CAP = 4
NF = 16
NS = 8
ROWS = 8
MINE = 8
BLOCKS = 9
SPOTS = BLOCKS * 16
MESH = pl.DeviceIdType.MESH
F32 = jnp.float32
BF16 = jnp.bfloat16


def split_halves(table):
    high = table.astype(np.float32).astype(jnp.bfloat16)
    low = (table - high.astype(np.float64)).astype(np.float32).astype(jnp.bfloat16)
    return high, low


def make_tables():
    k = np.arange(64)
    u = np.arange(32)
    b = np.arange(128)
    tau = 2.0 * np.pi
    first = tau * ((2 * k[:, None] * u[None, :]) % 64) / 64
    twist = tau * ((k[:, None] * b[None, :]) % FL) / FL
    last = tau * ((k[:, None] * b[None, :]) % 64) / 64
    scale = 1.0 / math.sqrt(FL)
    c, s = np.cos(first) * scale, np.sin(first) * scale
    ahead = np.concatenate(split_halves(np.block([[c, s], [-s, c]])), axis=1)
    cl, sl = np.cos(last), np.sin(last)
    frow = np.concatenate(split_halves(np.block([[cl, sl], [-sl, cl]])), axis=0)
    cb, sb = cl[:, :64].T, sl[:, :64].T
    brow = np.concatenate(split_halves(np.block([[cb, -sb], [sb, cb]])), axis=0)
    back = np.zeros((2, 2, 32, 2, 2, 64))
    for r in range(2):
        back[r, 0, :, 0, r], back[r, 0, :, 1, r] = c.T, -s.T
        back[r, 1, :, 0, r], back[r, 1, :, 1, r] = s.T, c.T
    back = np.concatenate(split_halves(back.reshape(128, 256)), axis=0)
    ct, st = np.cos(twist), np.sin(twist)
    twists = np.concatenate([ct, st, np.tile(ct.T, (1, 2)), np.tile(st.T, (1, 2))], axis=0).astype(np.float32)
    narrow = np.concatenate([ahead, brow], axis=0)
    wide = np.concatenate([frow, back], axis=0)
    return twists, narrow, wide


def mm(a, b):
    return jnp.dot(a, b, preferred_element_type=F32)


def mm_nt(a, b):
    return lax.dot_general(a, b, (((1,), (1,)), ((), ())), preferred_element_type=F32)


def halves(x):
    high = x.astype(BF16)
    return high, (x - high.astype(F32)).astype(BF16)


def iota(shape, dim):
    return lax.broadcasted_iota(jnp.int32, shape, dim)


def rows_of(*parts):
    return jnp.concatenate(parts, axis=0)


def lanes_of(*parts):
    return jnp.concatenate(parts, axis=1)


def both_parts(column):
    shaped = column.reshape(NF, MINE, 128)
    return jnp.concatenate([shaped, shaped], axis=1).reshape(256, 128)


def ones_where(mask):
    return jnp.where(mask, 1.0, 0.0).astype(BF16)


def kernel(
    fo_in, so_in, si_in, so_v_in, ow_v_in, strips_in, gw_in, twists_in, narrow_in, wide_in, screens, out,
    fo, so, si, so_v, ow_v, strips, gw, twists, narrow, wide, scr,
    xs, col, qsc, qfin, picks, spread, gather, low_mask, sbuf, rbuf, esend, ebuf,
    wmsg, wrows, wsend, wgot, wlow, whigh, tback, oscr,
    in_sem, scr_sem, s1, r1, s2, r2, sw1, rw1, sw2, rw2,
):
    f = lax.axis_index("facet")
    s = lax.axis_index("sub")
    fx, fy = f // 4, f % 4
    steps = [(dx, dy) for dx in range(4) for dy in range(4) if (dx, dy) != (0, 0)]
    steps.sort(key=lambda d: -(min(d[0], 4 - d[0]) + min(d[1], 4 - d[1])))
    peers = [((fx + dx) % 4) * 4 + (fy + dy) % 4 for dx, dy in steps]
    others = [(s + d) % NS for d in range(1, NS)]

    fetch = [
        pltpu.make_async_copy(a, b, in_sem.at[n])
        for n, (a, b) in enumerate(
            [
                (strips_in, strips), (so_v_in, so_v), (ow_v_in, ow_v), (narrow_in, narrow), (twists_in, twists),
                (wide_in, wide), (gw_in, gw), (fo_in, fo), (so_in, so), (si_in, si),
            ]
        )
    ]
    barrier = pltpu.get_barrier_semaphore()
    for p in peers:
        pl.semaphore_signal(barrier, inc=1, device_id=(p, s), device_id_type=MESH)
    for c in fetch:
        c.start()
    for t in others:
        pl.semaphore_signal(barrier, inc=1, device_id=(f, t), device_id_type=MESH)
    screen_copy = pltpu.make_async_copy(screens.at[:, pl.ds(pl.multiple_of(s * ROWS, ROWS), ROWS), :], scr, scr_sem)
    screen_copy.start()

    lane = iota((128, 128), 1)
    lane4 = iota((256, 128), 1)
    part4 = (iota((256, 128), 0) >> 3) & 1
    for c in fetch:
        c.wait()

    so_col = jnp.transpose(jnp.broadcast_to(so_v[...], (128, 128)))
    ow_row = jnp.broadcast_to(ow_v[...], (128, 128))
    ow_col = jnp.transpose(ow_row)
    col[...] = so_col
    start_col = (so_col + fo[f]) & (FL - 1)
    q4 = both_parts(start_col >> 6)
    take_low = (lane4 & 63) >= both_parts(start_col & 63)
    picks[:256] = ones_where(lane4 == q4 + 64 * part4)
    picks[256:] = ones_where(lane4 == ((q4 + 1) & 63) + 64 * part4)

    tf_high = mm(picks[...], wide[:128]).astype(BF16)
    tf_low = mm(picks[...], wide[128:256]).astype(BF16)
    for v in range(64):
        xs[pl.ds(8 * v, 8), :] = strips[:, 128 * v : 128 * v + 128].astype(F32)
    tc = lanes_of(twists[:64], twists[:64])
    ts = lanes_of(twists[64:128], twists[64:128])

    for h in range(2):
        columns = []
        for pair in (2 * h, 2 * h + 1):
            x = lanes_of(xs[pl.ds(2 * pair, 64, stride=8), :], xs[pl.ds(2 * pair + 1, 64, stride=8), :]).astype(BF16)
            a = mm(narrow[:128], rows_of(x, x))
            re, im = a[:64], a[64:]
            b_re = re * tc + im * ts
            b_im = im * tc - re * ts
            columns += [lanes_of(b_re[:, :128], b_im[:, :128]), lanes_of(b_re[:, 128:], b_im[:, 128:])]
        b_high, b_low = halves(rows_of(*columns))
        g = mm_nt(tf_high, b_high) + mm_nt(tf_low, b_high) + mm_nt(tf_high, b_low)
        for n in range(2):
            block = slice(128 * n, 128 * n + 128)
            piece = jnp.where(take_low, g[:256, block], g[256:, block]).astype(BF16)
            sbuf[:, 2 * h + n] = piece.reshape(NF, 16, 128)
    rbuf[pl.ds(f, 1)] = sbuf[pl.ds(f, 1)]

    for q in range(4):
        wmsg[pl.ds(4 * q, 4), :] = gw[:, 128 * q : 128 * q + 128]
    wrows[pl.ds(s, 1)] = wmsg[...].astype(BF16)[None]

    pl.semaphore_wait(barrier, NF - 1 + NS - 1)

    def remote(src, dst, send, recv, to):
        return pltpu.make_async_remote_copy(
            src_ref=src, dst_ref=dst, send_sem=send, recv_sem=recv, device_id=to, device_id_type=MESH
        )

    def everything(buffer, send, recv):
        return remote(buffer, buffer, send, recv, (peers[0], s))

    for p in peers:
        remote(sbuf.at[p], rbuf.at[f], s1, r1, (p, s)).start()
    for t in others:
        remote(wrows.at[s], wrows.at[s], sw1, rw1, (f, t)).start()

    tback[...] = mm_nt(narrow[128:], picks[...]).astype(BF16)

    lane8 = iota((8, 128), 1)
    left = lane8 < 64
    base = pl.multiple_of(f * MINE, MINE)
    r8 = col[pl.ds(base, MINE), :] & 63
    zero = jnp.zeros((8, 128), F32)
    screen_copy.wait()
    for j in range(MINE):
        shift = so[base + j] & 63
        screen = scr[si[base + j]].astype(F32)
        for part in range(2):
            rolled = [
                pltpu.roll(screen[:, 512 * part + 128 * v : 512 * part + 128 * v + 128], shift, 1) for v in range(4)
            ]
            rolled = [zero] + rolled + [zero]
            for v in range(5):
                piece = jnp.where(lane8 >= shift, rolled[v + 1], rolled[v])
                other = pltpu.roll(piece, 64, 1)
                qsc[part, 2 * v, pl.ds(j, ROWS, stride=MINE), :] = jnp.where(left, piece, other)
                if 2 * v + 1 < BLOCKS:
                    qsc[part, 2 * v + 1, pl.ds(j, ROWS, stride=MINE), :] = jnp.where(left, other, piece)
    for part in range(2):
        for b in range(BLOCKS):
            for pair in range(4):
                at = 16 * pair
                qfin[part, b, :, pl.ds(128 * pair, 128)] = jnp.where(
                    left, qsc[part, b, pl.ds(at, 8), :], qsc[part, b, pl.ds(at + 8, 8), :]
                )

    lane256 = iota((8, 256), 1)
    own = iota((8, 256), 0)
    r8w = lanes_of(r8, r8)
    for n in range(NF):
        first = ((r8w + fo[n]) >> 6) * 16 + own
        for late in range(2):
            spot = first + 16 * late
            at = 256 * late + 16 * n
            spread[pl.ds(at, 16), :] = rows_of(
                jnp.where(lane256 == spot, 1.0, 0.0), jnp.where(lane256 == spot + 8, 1.0, 0.0)
            ).astype(BF16)
        mask = jnp.where((lane8 & 63) >= ((r8 + fo[n]) & 63), 1.0, 0.0)
        low_mask[n] = rows_of(mask, mask).astype(BF16)
    unit = ones_where(iota((SPOTS, 256), 0) == iota((SPOTS, 256), 1))
    gather[...] = mm_nt(unit, spread[...]).astype(BF16)

    remote(wrows.at[pl.ds(0, NS - 1)], wrows.at[pl.ds(0, NS - 1)], sw1, rw1, (f, others[0])).wait_recv()
    all_rows = wrows[...].reshape(128, 128)
    lane64 = iota((64, 128), 1)
    sub64 = iota((64, 128), 0)
    gap = lane64 - (16 * ((sub64 >> 2) & 7) + 4 * (sub64 >> 5) + (sub64 & 3))
    lane32 = iota((32, 128), 1)
    for n in range(NF):
        offset = fo[n]
        shift = offset & 127
        rows = mm(ones_where(gap == 4 * (offset >> 7)), all_rows)
        turn = (128 - shift) & 127
        window = jnp.where(lane32 < 128 - shift, pltpu.roll(rows[:32], turn, 1), pltpu.roll(rows[32:], turn, 1))
        packed = jnp.where(lane32[:16] < 64, window[:16], pltpu.roll(window[16:], 64, 1))
        wsend[n] = packed.astype(BF16)
    wgot[pl.ds(f, 1)] = wsend[pl.ds(f, 1)]
    for p in peers:
        remote(wsend.at[p], wgot.at[f], sw2, rw2, (p, s)).start()

    everything(rbuf.at[pl.ds(0, NF - 1)], s1, r1).wait_recv()

    nothing = jnp.zeros((256 - SPOTS, 256), BF16)
    for h in range(2):
        low, high = [], []
        for pair in (2 * h, 2 * h + 1):
            c = rbuf[:, pair]
            c_low = c * low_mask[...]
            low.append(c_low.reshape(256, 128))
            high.append((c - c_low).reshape(256, 128))
        sums = mm(gather[...], rows_of(lanes_of(*low), lanes_of(*high)))
        done = []
        lanes = pl.ds(256 * h, 256)
        for b in range(BLOCKS):
            re, im = sums[16 * b : 16 * b + 8], sums[16 * b + 8 : 16 * b + 16]
            cs, sn = qfin[0, b, :, lanes], qfin[1, b, :, lanes]
            done += [re * cs - im * sn, re * sn + im * cs]
        both = mm(spread[...], rows_of(rows_of(*done).astype(BF16), nothing))
        keep = low_mask[...].reshape(256, 128) > 0
        for n in range(2):
            block = slice(128 * n, 128 * n + 128)
            piece = jnp.where(keep, both[:256, block], both[256:, block]).astype(BF16)
            esend[h, :, n] = piece.reshape(NF, 16, 128)
        for p in peers:
            remote(esend.at[h, p], ebuf.at[h, f], s2.at[h], r2.at[h], (p, s)).start()
    ebuf[:, pl.ds(f, 1)] = esend[:, pl.ds(f, 1)]

    everything(wgot.at[pl.ds(0, NF - 1)], sw2, rw2).wait_recv()
    ow_row = jnp.broadcast_to(ow_v[...], (128, 128))
    ow_col = jnp.transpose(ow_row)
    earlier = jnp.where((ow_row == ow_col) & (lane < iota((128, 128), 0)), 1.0, 0.0)
    slot = jnp.sum(earlier, axis=1, keepdims=True).astype(jnp.int32)
    weight_row = ow_col * CAP + slot
    spot = 16 * (weight_row >> 5) + (weight_row & 15)
    lane_w = iota((128, 256), 1)
    rows = mm(ones_where(lane_w == lanes_of(spot, spot)), wgot[...].reshape(256, 128))
    upper = ((weight_row >> 4) & 1) == 1
    weight = jnp.where((lane < 64) != upper, rows, pltpu.roll(rows, 64, 1))
    r_col = (col[...] + fo[f]) & 63
    for bit in range(6):
        amount = 1 << bit
        weight = jnp.where((r_col & amount) != 0, pltpu.roll(weight, amount, 1), weight)
    weight4 = both_parts(weight)
    first4 = (lane4 & 63) >= both_parts(r_col)
    wlow[...] = jnp.where(first4, weight4, 0.0).astype(BF16).reshape(NF, 16, 128)
    whigh[...] = jnp.where(first4, 0.0, weight4).astype(BF16).reshape(NF, 16, 128)

    for h in range(2):
        everything(ebuf.at[h, pl.ds(0, NF - 1)], s2.at[h], r2.at[h]).wait_recv()
        low, high = [], []
        for n in range(2):
            e = ebuf[h, :, n]
            low.append((e * wlow[...]).reshape(256, 128))
            high.append((e * whigh[...]).reshape(256, 128))
        d = mm(tback[...], rows_of(lanes_of(*low), lanes_of(*high)))
        d = d[:128] + d[128:]
        re, im = d[:64], d[64:]
        d_re, d_im = [], []
        for turn in range(2):
            at = pl.ds(128 + 64 * turn, 64)
            cs = lanes_of(twists[at, :], twists[at, :])
            at = pl.ds(256 + 64 * turn, 64)
            sn = lanes_of(twists[at, :], twists[at, :])
            d_re.append(re * cs - im * sn)
            d_im.append(re * sn + im * cs)
        d_re, d_im = rows_of(*d_re), rows_of(*d_im)
        d_high, d_low = halves(
            rows_of(lanes_of(d_re[:, :128], d_im[:, :128]), lanes_of(d_re[:, 128:], d_im[:, 128:]))
        )
        o = mm_nt(wide[256:], d_high)
        o = o[:128] + o[128:] + mm_nt(wide[256:384], d_low)
        for n in range(2):
            for r in range(2):
                oscr[pl.ds(4 * h + 2 * n + r, 64, stride=8), :] = o[64 * r : 64 * r + 64, 128 * n : 128 * n + 128]
    for v in range(64):
        out[:, 128 * v : 128 * v + 128] = oscr[pl.ds(8 * v, 8), :]

    everything(sbuf.at[pl.ds(0, NF - 1)], s1, r1).wait_send()
    everything(wsend.at[pl.ds(0, NF - 1)], sw2, rw2).wait_send()
    remote(wrows.at[pl.ds(0, NS - 1)], wrows.at[pl.ds(0, NS - 1)], sw1, rw1, (f, others[0])).wait_send()
    for h in range(2):
        everything(esend.at[h, pl.ds(0, NF - 1)], s2.at[h], r2.at[h]).wait_send()


def local(strips, facet_offset, subgrid_offset, owner, screen_index, screens, grid_weight):
    twists, narrow, wide = [jnp.asarray(t) for t in make_tables()]
    dma = pltpu.SemaphoreType.DMA
    result = pl.pallas_call(
        kernel,
        out_shape=jax.ShapeDtypeStruct((ROWS, 2 * FL), F32),
        in_specs=[pl.BlockSpec(memory_space=pl.ANY)] * 11,
        out_specs=pl.BlockSpec(memory_space=pltpu.VMEM),
        scratch_shapes=[
            pltpu.SMEM((16,), jnp.int32),
            pltpu.SMEM((128,), jnp.int32),
            pltpu.SMEM((128,), jnp.int32),
            pltpu.VMEM((1, 128), jnp.int32),
            pltpu.VMEM((1, 128), jnp.int32),
            pltpu.VMEM((ROWS, 2 * FL), BF16),
            pltpu.VMEM((CAP, 512), F32),
            pltpu.VMEM((384, 128), F32),
            pltpu.VMEM((384, 128), BF16),
            pltpu.VMEM((512, 256), BF16),
            pltpu.VMEM((16, ROWS, 1024), BF16),
            pltpu.VMEM((576, 128), F32),
            pltpu.VMEM((128, 128), jnp.int32),
            pltpu.VMEM((2, BLOCKS + 1, 128, 128), F32),
            pltpu.VMEM((2, BLOCKS, 8, 512), F32),
            pltpu.VMEM((512, 128), BF16),
            pltpu.VMEM((512, 256), BF16),
            pltpu.VMEM((SPOTS, 512), BF16),
            pltpu.VMEM((NF, 16, 128), BF16),
            pltpu.VMEM((NF, 4, 16, 128), BF16),
            pltpu.VMEM((NF, 4, 16, 128), BF16),
            pltpu.VMEM((2, NF, 2, 16, 128), BF16),
            pltpu.VMEM((2, NF, 2, 16, 128), BF16),
            pltpu.VMEM((16, 128), F32),
            pltpu.VMEM((NS, 16, 128), BF16),
            pltpu.VMEM((NF, 16, 128), BF16),
            pltpu.VMEM((NF, 16, 128), BF16),
            pltpu.VMEM((NF, 16, 128), BF16),
            pltpu.VMEM((NF, 16, 128), BF16),
            pltpu.VMEM((256, 512), BF16),
            pltpu.VMEM((576, 128), F32),
            dma((10,)), dma, dma, dma, dma((2,)), dma((2,)), dma, dma, dma, dma,
        ],
        compiler_params=pltpu.CompilerParams(collective_id=0, has_side_effects=True),
        name="round_trip",
    )(
        facet_offset,
        subgrid_offset,
        screen_index,
        subgrid_offset.reshape(1, -1),
        owner.reshape(1, -1),
        strips[0],
        grid_weight,
        twists,
        narrow,
        wide,
        screens,
    )
    return result[None]


def solution(mesh):
    in_specs = (P("facet", "sub", None), P(), P(), P(), P(), P(), P(("facet", "sub"), None))
    out_specs = P("facet", "sub", None)
    return jax.shard_map(local, mesh=mesh, in_specs=in_specs, out_specs=out_specs, check_vma=False)
```

time: 1260 us -> 21.7 us (0.02)
  other arithmetic: 680 us -> 0 us
  matrix products: 418 us -> 0 us
  local copies, waits for them, and re-layouts: 105 us -> 1.67 us
  waiting for transfers between devices: 31.5 us -> 0 us
  Pallas kernels: 0 us -> 19.8 us
  starting transfers between devices: 16.1 us -> 0 us
    another operation x18 -> x0, other arithmetic: 583 us -> none
    dot_general x18 -> x0, matrix products: 418 us -> none  [the longest x8 292 us: add_block(): lax.dot_general(piece, block, (((1,), (1,)), ((), ())), preferred_element...]
    unnamed x6 -> x0, other arithmetic: 90.7 us -> none
    gather x7 -> x0, local copies, waits for them, and re-layouts: 66.3 us -> none  [the longest x2 31.8 us: local(): imag_part = spectrum[:, FL + chosen_freq]]
    all_to_all x2 -> x0, waiting for transfers between devices: 31.5 us -> none  [the longest x1 18.9 us: send_back(): lax.all_to_all(buffer, ('facet', 'sub'), split_axis=0, concat_axis=0, til...]
    pallas_call x0 -> x1, Pallas kernels: none -> 19.8 us  [local(): pl.pallas_call(kernel, out_shape=jax.ShapeDtypeStruct((ROWS, 2 * FL), F32...]
    all_to_all x2 -> x0, starting transfers between devices: 16.1 us -> none  [the longest x1 11.5 us: send_forward(): lax.all_to_all(buffer, ('facet', 'sub'), split_axis=0, concat_axis=0, til...]
  transfers between devices with their start and end apart: 2 -> 0, of which waited for: 2 -> 0; matrix products, arithmetic and copies ran while one was open for 1% -> 0% of each run, Pallas kernels for 0% -> 0%
where the time goes in v2:
time: 21.7 us; the launch traced here: 21.5 us
  Pallas kernels  19.8 us (91%)
  local copies, waits for them, and re-layouts  1.67 us (8%)
    pallas_call x1, Pallas kernels, local(): pl.pallas_call(kernel, out_shape=jax.ShapeDtypeStruct((ROWS, 2 * FL), F32...  19.8 us
    unnamed x1, local copies, waits for them, and re-layouts  1.67 us

profile of v2, /device:TPU:1, one launch (start us, length us, event | category | flops | bytes accessed | tf_op | source)
XLA Modules:
  0.0 21.5 jit_solution(8363267149108721316)
XLA Ops:
  0.0 19.8 %round_trip.1 = f32[8,8192]{1,0:T(8,128)} custom-call(s32[16]{0:T(128)} %fo_in.1, s32[128]{0:T(128)} %so_in.1, s32[128]{0:T(128)} %si_in.1, s32[1,128]{1,0:T(1,128)} %bitcast.6, s32[1,128]{1,0:T(1,128)} %bitcast.7, bf16[8,8192]{1,0:T(8,128)(2,1)} %bitcast.5, f32[4,512]{1,0:T(4,128)} %gw_in.1, f32[384,128]{1,0:T(8,128)} %constant.6.clone.twists_in, ...), custom_call_target="tpu_custom_call" | custom-call | tf_op jit(solution)/shard_map/round_trip/pallas_call | solution.py:335
  19.8 1.7 %copy.12 = f32[1,8,8192]{2,1,0:T(8,128)} copy(f32[1,8,8192]{2,1,0:T(8,128)} %bitcast.4) | data formatting | bytes 524288

commit v3 on v2

--- a/solution.py
+++ b/solution.py
@@ -335,7 +335,7 @@
     result = pl.pallas_call(
         kernel,
         out_shape=jax.ShapeDtypeStruct((ROWS, 2 * FL), F32),
-        in_specs=[pl.BlockSpec(memory_space=pl.ANY)] * 11,
+        in_specs=[pl.BlockSpec(memory_space=pltpu.HBM)] * 11,
         out_specs=pl.BlockSpec(memory_space=pltpu.VMEM),
         scratch_shapes=[
             pltpu.SMEM((16,), jnp.int32),
@@ -371,20 +371,16 @@
             pltpu.VMEM((576, 128), F32),
             dma((10,)), dma, dma, dma, dma((2,)), dma((2,)), dma, dma, dma, dma,
         ],
-        compiler_params=pltpu.CompilerParams(collective_id=0, has_side_effects=True),
+        compiler_params=pltpu.CompilerParams(collective_id=0, has_side_effects=True, vmem_limit_bytes=16*1024*1024),
         name="round_trip",
     )(
-        facet_offset,
-        subgrid_offset,
-        screen_index,
-        subgrid_offset.reshape(1, -1),
-        owner.reshape(1, -1),
-        strips[0],
-        grid_weight,
-        twists,
-        narrow,
-        wide,
-        screens,
+        *[
+            pltpu.with_memory_space_constraint(a, pltpu.HBM)
+            for a in (
+                facet_offset, subgrid_offset, screen_index, subgrid_offset.reshape(1, -1), owner.reshape(1, -1),
+                strips[0], grid_weight, twists, narrow, wide, screens,
+            )
+        ]
     )
     return result[None]
 

time: 21.7 us -> 20 us (0.922)
  local copies, waits for them, and re-layouts: 1.67 us -> 0.71 us
  Pallas kernels: 19.8 us -> 19.1 us
    unnamed x1, local copies, waits for them, and re-layouts: 1.67 us -> 0.71 us
    pallas_call x1, Pallas kernels: 19.8 us -> 19.1 us  [local(): pl.pallas_call(kernel, out_shape=jax.ShapeDtypeStruct((ROWS, 2 * FL), F32...]
where the time goes in v3:
time: 20 us; the launch traced here: 19.9 us
  Pallas kernels  19.1 us (96%)
  local copies, waits for them, and re-layouts  0.71 us (4%)
    pallas_call x1, Pallas kernels, local(): pl.pallas_call(kernel, out_shape=jax.ShapeDtypeStruct((ROWS, 2 * FL), F32...  19.1 us
    unnamed x1, local copies, waits for them, and re-layouts  0.71 us

profile of v3, /device:TPU:1, one launch (start us, length us, event | category | flops | bytes accessed | tf_op | source)
XLA Modules:
  0.0 19.9 jit_solution(6424926992214537958)
XLA Ops:
  0.0 19.1 %round_trip.1 = f32[8,8192]{1,0:T(8,128)S(1)} custom-call(s32[16]{0:T(128)} %fo_in.1, s32[128]{0:T(128)} %so_in.1, s32[128]{0:T(128)} %si_in.1, s32[1,128]{1,0:T(1,128)} %bitcast.6, s32[1,128]{1,0:T(1,128)} %bitcast.7, bf16[8,8192]{1,0:T(8,128)(2,1)} %bitcast.5, f32[4,512]{1,0:T(4,128)} %gw_in.1, f32[384,128]{1,0:T(8,128)} %constant.6.clone.twists_in, ...), custom_call_target="tpu_custom_call" | custom-call | tf_op jit(solution)/shard_map/round_trip/pallas_call | solution.py:335
  19.2 0.7 %copy.12 = f32[1,8,8192]{2,1,0:T(8,128)} copy(f32[1,8,8192]{2,1,0:T(8,128)S(1)} %bitcast.4) | data formatting | bytes 524288

commit v4 on v3

--- a/solution.py
+++ b/solution.py
@@ -90,10 +90,10 @@
 
 def kernel(
     fo_in, so_in, si_in, so_v_in, ow_v_in, strips_in, gw_in, twists_in, narrow_in, wide_in, screens, out,
-    fo, so, si, so_v, ow_v, strips, gw, twists, narrow, wide, scr,
+    fo, so, si, so_v, ow_v, strips, gw, gwq, twists, narrow, wide, scr,
     xs, col, qsc, qfin, picks, spread, gather, low_mask, sbuf, rbuf, esend, ebuf,
-    wmsg, wrows, wsend, wgot, wlow, whigh, tback, oscr,
-    in_sem, scr_sem, s1, r1, s2, r2, sw1, rw1, sw2, rw2,
+    wout, wgot, chosen, wlow, whigh, tback, oscr,
+    in_sem, scr_sem, known, s1, r1, s2, r2, sw1, rw1, sw2, rw2,
 ):
     f = lax.axis_index("facet")
     s = lax.axis_index("sub")
@@ -101,7 +101,6 @@
     steps = [(dx, dy) for dx in range(4) for dy in range(4) if (dx, dy) != (0, 0)]
     steps.sort(key=lambda d: -(min(d[0], 4 - d[0]) + min(d[1], 4 - d[1])))
     peers = [((fx + dx) % 4) * 4 + (fy + dy) % 4 for dx, dy in steps]
-    others = [(s + d) % NS for d in range(1, NS)]
 
     fetch = [
         pltpu.make_async_copy(a, b, in_sem.at[n])
@@ -117,8 +116,12 @@
         pl.semaphore_signal(barrier, inc=1, device_id=(p, s), device_id_type=MESH)
     for c in fetch:
         c.start()
-    for t in others:
+
+    def greet(t, carry):
         pl.semaphore_signal(barrier, inc=1, device_id=(f, t), device_id_type=MESH)
+        return carry
+
+    lax.fori_loop(s + 1, NS, greet, 0)
     screen_copy = pltpu.make_async_copy(screens.at[:, pl.ds(pl.multiple_of(s * ROWS, ROWS), ROWS), :], scr, scr_sem)
     screen_copy.start()
 
@@ -162,11 +165,22 @@
             sbuf[:, 2 * h + n] = piece.reshape(NF, 16, 128)
     rbuf[pl.ds(f, 1)] = sbuf[pl.ds(f, 1)]
 
+    lane_cap = iota((8, 128), 1)
+    gwq[...] = jnp.zeros((5, 8, 128), F32)
     for q in range(4):
-        wmsg[pl.ds(4 * q, 4), :] = gw[:, 128 * q : 128 * q + 128]
-    wrows[pl.ds(s, 1)] = wmsg[...].astype(BF16)[None]
-
-    pl.semaphore_wait(barrier, NF - 1 + NS - 1)
+        gwq[q, pl.ds(0, CAP), :] = gw[:, 128 * q : 128 * q + 128]
+    for n in range(NF):
+        shift = fo[n] & 127
+        block = fo[n] >> 7
+        turn = (128 - shift) & 127
+        window = jnp.where(
+            lane_cap < 128 - shift, pltpu.roll(gwq[block], turn, 1), pltpu.roll(gwq[block + 1], turn, 1)
+        )
+        beside = pltpu.roll(pltpu.roll(window, 6, 0), 64, 1)
+        wout[n] = jnp.where(lane_cap < 64, window, beside)[:2].astype(BF16)
+    wgot[pl.ds(s, 1), pl.ds(f, 1)] = wout[pl.ds(f, 1)][None]
+
+    pl.semaphore_wait(barrier, NF - 1 + s)
 
     def remote(src, dst, send, recv, to):
         return pltpu.make_async_remote_copy(
@@ -177,9 +191,23 @@
         return remote(buffer, buffer, send, recv, (peers[0], s))
 
     for p in peers:
+        remote(wout.at[p], wgot.at[s, f], sw1, rw1, (p, s)).start()
+    for p in peers:
         remote(sbuf.at[p], rbuf.at[f], s1, r1, (p, s)).start()
-    for t in others:
-        remote(wrows.at[s], wrows.at[s], sw1, rw1, (f, t)).start()
+
+    def tell(t, carry):
+        pl.semaphore_signal(known.at[s], inc=1, device_id=(f, t), device_id_type=MESH)
+        return carry
+
+    def hear(t, carry):
+        pl.semaphore_wait(known.at[t], 1)
+        return carry
+
+    def weights_to(t, carry):
+        remote(wgot.at[s], wgot.at[s], sw2, rw2, (f, t)).start()
+        return carry
+
+    lax.fori_loop(0, s, tell, 0)
 
     tback[...] = mm_nt(narrow[128:], picks[...]).astype(BF16)
 
@@ -227,23 +255,8 @@
     unit = ones_where(iota((SPOTS, 256), 0) == iota((SPOTS, 256), 1))
     gather[...] = mm_nt(unit, spread[...]).astype(BF16)
 
-    remote(wrows.at[pl.ds(0, NS - 1)], wrows.at[pl.ds(0, NS - 1)], sw1, rw1, (f, others[0])).wait_recv()
-    all_rows = wrows[...].reshape(128, 128)
-    lane64 = iota((64, 128), 1)
-    sub64 = iota((64, 128), 0)
-    gap = lane64 - (16 * ((sub64 >> 2) & 7) + 4 * (sub64 >> 5) + (sub64 & 3))
-    lane32 = iota((32, 128), 1)
-    for n in range(NF):
-        offset = fo[n]
-        shift = offset & 127
-        rows = mm(ones_where(gap == 4 * (offset >> 7)), all_rows)
-        turn = (128 - shift) & 127
-        window = jnp.where(lane32 < 128 - shift, pltpu.roll(rows[:32], turn, 1), pltpu.roll(rows[32:], turn, 1))
-        packed = jnp.where(lane32[:16] < 64, window[:16], pltpu.roll(window[16:], 64, 1))
-        wsend[n] = packed.astype(BF16)
-    wgot[pl.ds(f, 1)] = wsend[pl.ds(f, 1)]
-    for p in peers:
-        remote(wsend.at[p], wgot.at[f], sw2, rw2, (p, s)).start()
+    everything(wgot.at[0, pl.ds(0, NF - 1)], sw1, rw1).wait_recv()
+    lax.fori_loop(0, s, weights_to, 0)
 
     everything(rbuf.at[pl.ds(0, NF - 1)], s1, r1).wait_recv()
 
@@ -272,18 +285,21 @@
             remote(esend.at[h, p], ebuf.at[h, f], s2.at[h], r2.at[h], (p, s)).start()
     ebuf[:, pl.ds(f, 1)] = esend[:, pl.ds(f, 1)]
 
-    everything(wgot.at[pl.ds(0, NF - 1)], sw2, rw2).wait_recv()
+    lax.fori_loop(s + 1, NS, hear, 0)
+    lax.fori_loop(s + 1, NS, weights_to, 0)
+
     ow_row = jnp.broadcast_to(ow_v[...], (128, 128))
     ow_col = jnp.transpose(ow_row)
     earlier = jnp.where((ow_row == ow_col) & (lane < iota((128, 128), 0)), 1.0, 0.0)
     slot = jnp.sum(earlier, axis=1, keepdims=True).astype(jnp.int32)
     weight_row = ow_col * CAP + slot
-    spot = 16 * (weight_row >> 5) + (weight_row & 15)
-    lane_w = iota((128, 256), 1)
-    rows = mm(ones_where(lane_w == lanes_of(spot, spot)), wgot[...].reshape(256, 128))
-    upper = ((weight_row >> 4) & 1) == 1
+    spot = 32 * ((weight_row >> 2) & 7) + 2 * (weight_row >> 5) + (weight_row & 1)
+    chosen[...] = ones_where(iota((128, 256), 1) == lanes_of(spot, spot))
+    upper = (weight_row & 2) == 2
+    r_col = (col[...] + fo[f]) & 63
+    everything(wgot.at[pl.ds(0, NS - 1)], sw2, rw2).wait_recv()
+    rows = mm(chosen[...], wgot[...].reshape(256, 128))
     weight = jnp.where((lane < 64) != upper, rows, pltpu.roll(rows, 64, 1))
-    r_col = (col[...] + fo[f]) & 63
     for bit in range(6):
         amount = 1 << bit
         weight = jnp.where((r_col & amount) != 0, pltpu.roll(weight, amount, 1), weight)
@@ -323,8 +339,8 @@
         out[:, 128 * v : 128 * v + 128] = oscr[pl.ds(8 * v, 8), :]
 
     everything(sbuf.at[pl.ds(0, NF - 1)], s1, r1).wait_send()
-    everything(wsend.at[pl.ds(0, NF - 1)], sw2, rw2).wait_send()
-    remote(wrows.at[pl.ds(0, NS - 1)], wrows.at[pl.ds(0, NS - 1)], sw1, rw1, (f, others[0])).wait_send()
+    everything(wout.at[pl.ds(0, NF - 1)], sw1, rw1).wait_send()
+    everything(wgot.at[pl.ds(0, NS - 1)], sw2, rw2).wait_send()
     for h in range(2):
         everything(esend.at[h, pl.ds(0, NF - 1)], s2.at[h], r2.at[h]).wait_send()
 
@@ -345,6 +361,7 @@
             pltpu.VMEM((1, 128), jnp.int32),
             pltpu.VMEM((ROWS, 2 * FL), BF16),
             pltpu.VMEM((CAP, 512), F32),
+            pltpu.VMEM((5, 8, 128), F32),
             pltpu.VMEM((384, 128), F32),
             pltpu.VMEM((384, 128), BF16),
             pltpu.VMEM((512, 256), BF16),
@@ -361,15 +378,14 @@
             pltpu.VMEM((NF, 4, 16, 128), BF16),
             pltpu.VMEM((2, NF, 2, 16, 128), BF16),
             pltpu.VMEM((2, NF, 2, 16, 128), BF16),
-            pltpu.VMEM((16, 128), F32),
-            pltpu.VMEM((NS, 16, 128), BF16),
-            pltpu.VMEM((NF, 16, 128), BF16),
-            pltpu.VMEM((NF, 16, 128), BF16),
+            pltpu.VMEM((NF, 2, 128), BF16),
+            pltpu.VMEM((NS, NF, 2, 128), BF16),
+            pltpu.VMEM((128, 256), BF16),
             pltpu.VMEM((NF, 16, 128), BF16),
             pltpu.VMEM((NF, 16, 128), BF16),
             pltpu.VMEM((256, 512), BF16),
             pltpu.VMEM((576, 128), F32),
-            dma((10,)), dma, dma, dma, dma((2,)), dma((2,)), dma, dma, dma, dma,
+            dma((10,)), dma, pltpu.SemaphoreType.REGULAR((NS,)), dma, dma, dma((2,)), dma((2,)), dma, dma, dma, dma,
         ],
         compiler_params=pltpu.CompilerParams(collective_id=0, has_side_effects=True, vmem_limit_bytes=16*1024*1024),
         name="round_trip",

time: 20 us -> 19.3 us (0.965)
  Pallas kernels: 19.1 us -> 18.5 us
    pallas_call x1, Pallas kernels: 19.1 us -> 18.5 us  [local(): pl.pallas_call(kernel, out_shape=jax.ShapeDtypeStruct((ROWS, 2 * FL), F32...]
where the time goes in v4:
time: 19.3 us; the launch traced here: 19.2 us
  Pallas kernels  18.5 us (96%)
  local copies, waits for them, and re-layouts  0.71 us (4%)
    pallas_call x1, Pallas kernels, local(): pl.pallas_call(kernel, out_shape=jax.ShapeDtypeStruct((ROWS, 2 * FL), F32...  18.5 us
    unnamed x1, local copies, waits for them, and re-layouts  0.71 us

profile of v4, /device:TPU:1, one launch (start us, length us, event | category | flops | bytes accessed | tf_op | source)
XLA Modules:
  0.0 19.2 jit_solution(15714524378558210719)
XLA Ops:
  0.0 18.5 %round_trip.1 = f32[8,8192]{1,0:T(8,128)S(1)} custom-call(s32[16]{0:T(128)} %fo_in.1, s32[128]{0:T(128)} %so_in.1, s32[128]{0:T(128)} %si_in.1, s32[1,128]{1,0:T(1,128)} %bitcast.6, s32[1,128]{1,0:T(1,128)} %bitcast.7, bf16[8,8192]{1,0:T(8,128)(2,1)} %bitcast.5, f32[4,512]{1,0:T(4,128)} %gw_in.1, f32[384,128]{1,0:T(8,128)} %constant.6.clone.twists_in, ...), custom_call_target="tpu_custom_call" | custom-call | tf_op jit(solution)/shard_map/round_trip/pallas_call | solution.py:351
  18.5 0.7 %copy.12 = f32[1,8,8192]{2,1,0:T(8,128)} copy(f32[1,8,8192]{2,1,0:T(8,128)S(1)} %bitcast.4) | data formatting | bytes 524288

commit v5 on v4

--- a/solution.py
+++ b/solution.py
@@ -310,6 +310,7 @@
 
     for h in range(2):
         everything(ebuf.at[h, pl.ds(0, NF - 1)], s2.at[h], r2.at[h]).wait_recv()
+    for h in range(2):
         low, high = [], []
         for n in range(2):
             e = ebuf[h, :, n]

time: 19.3 us -> 19.1 us (0.990); the launches traced: 19.2 us -> 18.8 us
  Pallas kernels: 18.5 us -> 18 us
    pallas_call x1, Pallas kernels: 18.5 us -> 18 us  [local(): pl.pallas_call(kernel, out_shape=jax.ShapeDtypeStruct((ROWS, 2 * FL), F32...]
where the time goes in v5:
time: 19.1 us; the launch traced here: 18.8 us
  Pallas kernels  18 us (94%)
  local copies, waits for them, and re-layouts  0.71 us (4%)
    pallas_call x1, Pallas kernels, local(): pl.pallas_call(kernel, out_shape=jax.ShapeDtypeStruct((ROWS, 2 * FL), F32...  18 us
    unnamed x1, local copies, waits for them, and re-layouts  0.71 us

profile of v5, /device:TPU:1, one launch (start us, length us, event | category | flops | bytes accessed | tf_op | source)
XLA Modules:
  0.0 18.8 jit_solution(9951972370308100)
XLA Ops:
  0.0 18.0 %round_trip.1 = f32[8,8192]{1,0:T(8,128)S(1)} custom-call(s32[16]{0:T(128)} %fo_in.1, s32[128]{0:T(128)} %so_in.1, s32[128]{0:T(128)} %si_in.1, s32[1,128]{1,0:T(1,128)} %bitcast.6, s32[1,128]{1,0:T(1,128)} %bitcast.7, bf16[8,8192]{1,0:T(8,128)(2,1)} %bitcast.5, f32[4,512]{1,0:T(4,128)} %gw_in.1, f32[384,128]{1,0:T(8,128)} %constant.6.clone.twists_in, ...), custom_call_target="tpu_custom_call" | custom-call | tf_op jit(solution)/shard_map/round_trip/pallas_call | solution.py:352
  18.1 0.7 %copy.12 = f32[1,8,8192]{2,1,0:T(8,128)} copy(f32[1,8,8192]{2,1,0:T(8,128)S(1)} %bitcast.4) | data formatting | bytes 524288

commit v6 on v4

--- a/solution.py
+++ b/solution.py
@@ -281,8 +281,9 @@
             block = slice(128 * n, 128 * n + 128)
             piece = jnp.where(keep, both[:256, block], both[256:, block]).astype(BF16)
             esend[h, :, n] = piece.reshape(NF, 16, 128)
-        for p in peers:
-            remote(esend.at[h, p], ebuf.at[h, f], s2.at[h], r2.at[h], (p, s)).start()
+        if h == 1:
+            for p in peers:
+                remote(esend.at[:, p], ebuf.at[:, f], s2, r2, (p, s)).start()
     ebuf[:, pl.ds(f, 1)] = esend[:, pl.ds(f, 1)]
 
     lax.fori_loop(s + 1, NS, hear, 0)
@@ -308,8 +309,8 @@
     wlow[...] = jnp.where(first4, weight4, 0.0).astype(BF16).reshape(NF, 16, 128)
     whigh[...] = jnp.where(first4, 0.0, weight4).astype(BF16).reshape(NF, 16, 128)
 
+    everything(ebuf.at[:, pl.ds(0, NF - 1)], s2, r2).wait_recv()
     for h in range(2):
-        everything(ebuf.at[h, pl.ds(0, NF - 1)], s2.at[h], r2.at[h]).wait_recv()
         low, high = [], []
         for n in range(2):
             e = ebuf[h, :, n]
@@ -341,8 +342,7 @@
     everything(sbuf.at[pl.ds(0, NF - 1)], s1, r1).wait_send()
     everything(wout.at[pl.ds(0, NF - 1)], sw1, rw1).wait_send()
     everything(wgot.at[pl.ds(0, NS - 1)], sw2, rw2).wait_send()
-    for h in range(2):
-        everything(esend.at[h, pl.ds(0, NF - 1)], s2.at[h], r2.at[h]).wait_send()
+    everything(esend.at[:, pl.ds(0, NF - 1)], s2, r2).wait_send()
 
 
 def local(strips, facet_offset, subgrid_offset, owner, screen_index, screens, grid_weight):
@@ -385,7 +385,7 @@
             pltpu.VMEM((NF, 16, 128), BF16),
             pltpu.VMEM((256, 512), BF16),
             pltpu.VMEM((576, 128), F32),
-            dma((10,)), dma, pltpu.SemaphoreType.REGULAR((NS,)), dma, dma, dma((2,)), dma((2,)), dma, dma, dma, dma,
+            dma((10,)), dma, pltpu.SemaphoreType.REGULAR((NS,)), dma, dma, dma, dma, dma, dma, dma, dma,
         ],
         compiler_params=pltpu.CompilerParams(collective_id=0, has_side_effects=True, vmem_limit_bytes=16*1024*1024),
         name="round_trip",

time: 19.3 us -> 18.9 us (0.979)
  Pallas kernels: 18.5 us -> 18 us
    pallas_call x1, Pallas kernels: 18.5 us -> 18 us  [local(): pl.pallas_call(kernel, out_shape=jax.ShapeDtypeStruct((ROWS, 2 * FL), F32...]
where the time goes in v6:
time: 18.9 us; the launch traced here: 18.7 us
  Pallas kernels  18 us (95%)
  local copies, waits for them, and re-layouts  0.71 us (4%)
    pallas_call x1, Pallas kernels, local(): pl.pallas_call(kernel, out_shape=jax.ShapeDtypeStruct((ROWS, 2 * FL), F32...  18 us
    unnamed x1, local copies, waits for them, and re-layouts  0.71 us

profile of v6, /device:TPU:1, one launch (start us, length us, event | category | flops | bytes accessed | tf_op | source)
XLA Modules:
  0.0 18.7 jit_solution(5976951843858536781)
XLA Ops:
  0.0 18.0 %round_trip.1 = f32[8,8192]{1,0:T(8,128)S(1)} custom-call(s32[16]{0:T(128)} %fo_in.1, s32[128]{0:T(128)} %so_in.1, s32[128]{0:T(128)} %si_in.1, s32[1,128]{1,0:T(1,128)} %bitcast.6, s32[1,128]{1,0:T(1,128)} %bitcast.7, bf16[8,8192]{1,0:T(8,128)(2,1)} %bitcast.5, f32[4,512]{1,0:T(4,128)} %gw_in.1, f32[384,128]{1,0:T(8,128)} %constant.6.clone.twists_in, ...), custom_call_target="tpu_custom_call" | custom-call | tf_op jit(solution)/shard_map/round_trip/pallas_call | solution.py:351
  18.0 0.7 %copy.12 = f32[1,8,8192]{2,1,0:T(8,128)} copy(f32[1,8,8192]{2,1,0:T(8,128)S(1)} %bitcast.4) | data formatting | bytes 524288

commit v7 on v6

--- a/solution.py
+++ b/solution.py
@@ -92,7 +92,7 @@
     fo_in, so_in, si_in, so_v_in, ow_v_in, strips_in, gw_in, twists_in, narrow_in, wide_in, screens, out,
     fo, so, si, so_v, ow_v, strips, gw, gwq, twists, narrow, wide, scr,
     xs, col, qsc, qfin, picks, spread, gather, low_mask, sbuf, rbuf, esend, ebuf,
-    wout, wgot, chosen, wlow, whigh, tback, oscr,
+    wout, wgot, chosen, wlow, whigh, tback,
     in_sem, scr_sem, known, s1, r1, s2, r2, sw1, rw1, sw2, rw2,
 ):
     f = lax.axis_index("facet")
@@ -335,9 +335,7 @@
         o = o[:128] + o[128:] + mm_nt(wide[256:384], d_low)
         for n in range(2):
             for r in range(2):
-                oscr[pl.ds(4 * h + 2 * n + r, 64, stride=8), :] = o[64 * r : 64 * r + 64, 128 * n : 128 * n + 128]
-    for v in range(64):
-        out[:, 128 * v : 128 * v + 128] = oscr[pl.ds(8 * v, 8), :]
+                out[pl.ds(4 * h + 2 * n + r, 64, stride=8), :] = o[64 * r : 64 * r + 64, 128 * n : 128 * n + 128]
 
     everything(sbuf.at[pl.ds(0, NF - 1)], s1, r1).wait_send()
     everything(wout.at[pl.ds(0, NF - 1)], sw1, rw1).wait_send()
@@ -350,7 +348,7 @@
     dma = pltpu.SemaphoreType.DMA
     result = pl.pallas_call(
         kernel,
-        out_shape=jax.ShapeDtypeStruct((ROWS, 2 * FL), F32),
+        out_shape=jax.ShapeDtypeStruct((576, 128), F32),
         in_specs=[pl.BlockSpec(memory_space=pltpu.HBM)] * 11,
         out_specs=pl.BlockSpec(memory_space=pltpu.VMEM),
         scratch_shapes=[
@@ -384,7 +382,6 @@
             pltpu.VMEM((NF, 16, 128), BF16),
             pltpu.VMEM((NF, 16, 128), BF16),
             pltpu.VMEM((256, 512), BF16),
-            pltpu.VMEM((576, 128), F32),
             dma((10,)), dma, pltpu.SemaphoreType.REGULAR((NS,)), dma, dma, dma, dma, dma, dma, dma, dma,
         ],
         compiler_params=pltpu.CompilerParams(collective_id=0, has_side_effects=True, vmem_limit_bytes=16*1024*1024),
@@ -398,7 +395,7 @@
             )
         ]
     )
-    return result[None]
+    return result[:512].reshape(64, ROWS, 128).transpose(1, 0, 2).reshape(1, ROWS, 2 * FL)
 
 
 def solution(mesh):

time: 18.9 us -> 18.9 us (level)
    reshape x0 -> x1, local copies, waits for them, and re-layouts: none -> 0.72 us  [local(): result[:512].reshape(64, ROWS, 128).transpose(1, 0, 2)]
    unnamed x1 -> x0, local copies, waits for them, and re-layouts: 0.71 us -> none
where the time goes in v7:
time: 18.9 us; the launch traced here: 18.7 us
  Pallas kernels  18 us (95%)
  local copies, waits for them, and re-layouts  0.72 us (4%)
    pallas_call x1, Pallas kernels, local(): pl.pallas_call(kernel, out_shape=jax.ShapeDtypeStruct((576, 128), F32), i...  18 us
    reshape x1, local copies, waits for them, and re-layouts, local(): result[:512].reshape(64, ROWS, 128).transpose(1, 0, 2)  0.72 us

profile of v7, /device:TPU:1, one launch (start us, length us, event | category | flops | bytes accessed | tf_op | source)
XLA Modules:
  0.0 18.7 jit_solution(4872538536855067006)
XLA Ops:
  0.0 18.0 %round_trip.1 = f32[576,128]{1,0:T(8,128)S(1)} custom-call(s32[16]{0:T(128)} %fo_in.1, s32[128]{0:T(128)} %so_in.1, s32[128]{0:T(128)} %si_in.1, s32[1,128]{1,0:T(1,128)} %bitcast.10, s32[1,128]{1,0:T(1,128)} %bitcast.11, bf16[8,8192]{1,0:T(8,128)(2,1)} %bitcast.9, f32[4,512]{1,0:T(4,128)} %gw_in.1, f32[384,128]{1,0:T(8,128)} %constant.6.clone.twists_in, ...), custom_call_target="tpu_custom_call" | custom-call | tf_op jit(solution)/shard_map/round_trip/pallas_call | solution.py:349
  18.0 0.7 %slice_bitcast_fusion = f32[1,8,8192]{2,1,0:T(8,128)} fusion(f32[576,128]{1,0:T(8,128)S(1)} %round_trip.1), kind=kLoop, calls=%fused_computation | loop fusion | bytes 524288 | tf_op jit(solution)/shard_map/reshape | solution.py:398
